TPU v7x, 32 devices: a whole 2x2x4 slice. The times are simulated.
32 devices in a mesh: seq: 16 (over z, y, x), head: 2 (over core).
Axes of the slice: x: 2, y: 2, z: 4, core: 2. Of those that a mesh axis runs over, the one named last changes fastest.
Arguments:
- attn_q: bfloat16 [2048, 512], P('seq', 'head'), may hold values from -6 to 6
- attn_k: bfloat16 [2048, 512], P('seq', 'head'), may hold values from -6 to 6
- attn_v: bfloat16 [2048, 512], P('seq', 'head'), may hold values from -6 to 6
- attn_out: bfloat16 [2048, 512], P('seq', 'head'), may hold values from -0.29882812 to 0.29882812
- attn_dout: bfloat16 [2048, 512], P('seq', 'head'), may hold values from -96 to 96
- attn_lse: float32 [4, 2048], P('head', 'seq'), may hold values from 7 to 8
- w_kv: bfloat16 [512, 2, 512], P('seq', None, 'head'), may hold values from -0.25 to 0.25
- gdn_q: bfloat16 [2048, 512], P('seq', 'head'), may hold values from -6 to 6
- gdn_k: bfloat16 [2048, 512], P('seq', 'head'), may hold values from -6 to 6
- gdn_v: bfloat16 [2048, 512], P('seq', 'head'), may hold values from -6 to 6
- gdn_dout: bfloat16 [2048, 512], P('seq', 'head'), may hold values from -6 to 6
- gdn_log_decay: float32 [4, 2048], P('head', 'seq'), may hold values from -0.56 to 0
- gdn_beta: float32 [4, 2048], P('head', 'seq'), may hold values from 0 to 0.9
- gdn_states: float32 [32, 4, 128, 128], P('seq', 'head'), may hold values from -24 to 24
Outputs:
- attn_dq: bfloat16 [2048, 512], P('seq', 'head')
- attn_dx: bfloat16 [512, 2048], P('head', 'seq')
- gdn_dq: bfloat16 [2048, 512], P('seq', 'head')
- gdn_dk: bfloat16 [2048, 512], P('seq', 'head')
- gdn_dv: bfloat16 [2048, 512], P('seq', 'head')
- gdn_dlog_decay: float32 [4, 2048], P('head', 'seq')
- gdn_dbeta: float32 [4, 2048], P('head', 'seq')
All inputs are finite; a program needn't handle non-finite values.
Results may differ from a plain program's by a relative error of at most 0.0078.
Values may be sent and summed in bfloat16 or wider, within the bound.
A program may use at most 64 MiB of HBM per device.

v0:
```python
import functools
import jax
import jax.numpy as jnp
from jax import lax
from jax.experimental import pallas as pl
from jax.experimental.pallas import tpu as pltpu
from jax.sharding import PartitionSpec as P

BLOCK = 64
WINDOW = 1024
EPS = 1e-06
MESH = pl.DeviceIdType.MESH
F32 = jnp.float32
BF16 = jnp.bfloat16

NN = (((1,), (0,)), ((), ()))
NT = (((1,), (1,)), ((), ()))
TN = (((0,), (0,)), ((), ()))


def dot(left, right, dims=NN):
    return lax.dot_general(left, right, dims, preferred_element_type=F32)


def split(matrix):
    high = matrix.astype(BF16)
    return high, (matrix - high.astype(F32)).astype(BF16)


def mm(left, right, dims=NN):
    left_high, left_low = split(left)
    right_high, right_low = split(right)
    return dot(left_high, right_high, dims) + (
        dot(left_high, right_low, dims) + dot(left_low, right_high, dims)
    )


def mm_once(left, right, dims=NN):
    return dot(left.astype(BF16), right.astype(BF16), dims)


def mm_full(left, right, dims=NN):
    return lax.dot_general(
        left, right, dims, precision=lax.Precision.HIGHEST, preferred_element_type=F32
    )


def row_sum(matrix):
    return jnp.sum(matrix, axis=1, keepdims=True)


def column_sum(matrix):
    return jnp.sum(matrix, axis=0, keepdims=True)


def stack_heads(matrix, heads):
    depth = matrix.shape[1] // heads
    return jnp.concatenate([matrix[:, h * depth : (h + 1) * depth] for h in range(heads)], axis=0)


def group_size(count, reach):
    size = 1
    while size * size < count:
        size *= 2
    while count % size or reach % size:
        size //= 2
    return size


def kernel(
    n,
    head_n,
    q_ref, k_ref, v_ref, out_ref, dout_ref, lse_ref, w_ref,
    gq_ref, gk_ref, gv_ref, gdo_ref, decay_ref, beta_ref, states_ref,
    dq_out, dx_out, gdq_out, gdk_out, gdv_out, gdecay_out, gbeta_out,
    kv_buf, qd_buf, stat_own, stat_buf, w_all, ab_buf, carry_in, carry_out, dx_send, dx_recv,
    dq_acc, dkv_acc, map_buf,
    kv_send, kv_recv, qd_send, qd_recv, st_send, st_recv, w_send, w_recv,
    kv_pass, qd_pass, st_pass, w_pass,
    ab_send, ab_recv, c_send, c_recv, x_send, x_recv,
):
    me = lax.axis_index("seq")
    my_head = lax.axis_index("head")
    rows, columns = q_ref.shape
    heads = lse_ref.shape[0]
    depth = columns // heads
    reach = WINDOW // rows
    blocks = rows // BLOCK
    total = heads * rows
    size = group_size(n, WINDOW // rows)
    groups = n // size
    rank = lax.rem(me, size)
    group = lax.div(me, size)
    first = group * size

    barrier = pltpu.get_barrier_semaphore()
    for j in range(1, n):
        pl.semaphore_signal(
            barrier, inc=1, device_id={"seq": lax.rem(me + j, n)}, device_id_type=MESH
        )
    for j in range(1, head_n):
        pl.semaphore_signal(
            barrier, inc=1, device_id={"head": lax.rem(my_head + j, head_n)}, device_id_type=MESH
        )

    ones = jnp.ones((8, depth), F32)
    for h in range(heads):
        cols = slice(h * depth, (h + 1) * depth)
        product = dout_ref[:, cols].astype(F32) * out_ref[:, cols].astype(F32)
        stat_own[h : h + 1, :] = lse_ref[h : h + 1, :]
        stat_own[heads + h : heads + h + 1, :] = mm_full(ones, product, NT)[0:1, :]
    pl.semaphore_wait(barrier, n - 1 + head_n - 1)

    hops = min(reach // size, groups - 1)

    def move(source, target, sent, received, index):
        return pltpu.make_async_remote_copy(
            src_ref=source,
            dst_ref=target,
            send_sem=sent,
            recv_sem=received,
            device_id={"seq": index},
            device_id_type=MESH,
        )

    def kv_copies(j):
        index = lax.rem(me + j, n)
        return [
            move(
                (k_ref, v_ref)[i], kv_buf.at[j - 1, i],
                kv_send.at[j - 1, i], kv_recv.at[j - 1, i], index,
            )
            for i in range(2)
        ]

    def qd_copies(j):
        index = lax.rem(me + n - j, n)
        return [
            move(
                (q_ref, dout_ref)[i], qd_buf.at[j - 1, i],
                qd_send.at[j - 1, i], qd_recv.at[j - 1, i], index,
            )
            for i in range(2)
        ] + [move(stat_own, stat_buf.at[j - 1], st_send.at[j - 1], st_recv.at[j - 1], index)]

    def kv_passes(m, i):
        peer = lax.rem(rank + i, size)
        slot = m * size + peer - rank - 1
        return [
            move(
                kv_buf.at[m * size - 1, c], kv_buf.at[slot, c],
                kv_pass.at[m - 1, i, c], kv_recv.at[slot, c], first + peer,
            )
            for c in range(2)
        ]

    def qd_passes(m, i):
        peer = lax.rem(rank + i, size)
        slot = m * size + rank - peer - 1
        return [
            move(
                qd_buf.at[m * size - 1, c], qd_buf.at[slot, c],
                qd_pass.at[m - 1, i, c], qd_recv.at[slot, c], first + peer,
            )
            for c in range(2)
        ] + [
            move(
                stat_buf.at[m * size - 1], stat_buf.at[slot],
                st_pass.at[m - 1, i], st_recv.at[slot], first + peer,
            )
        ]

    def kv_goes(m, i):
        peer = lax.rem(rank + i, size)
        return (group >= m) & (m * size + peer - rank <= reach)

    def qd_goes(m, i):
        peer = lax.rem(rank + i, size)
        return (group + m < groups) & (m * size + rank - peer <= reach)

    w_rows = w_ref.shape[0]

    def w_copy(m):
        return move(
            w_ref, w_all.at[me], w_send.at[m - 1], w_recv.at[0, m], lax.rem(me + m * size, n)
        )

    def w_passes(i):
        peer = lax.rem(rank + i, size)
        return [
            move(
                w_ref if m == 0 else w_all.at[lax.rem(me + n - m * size, n)],
                w_all.at[lax.rem(me + n - m * size, n)],
                w_pass.at[i, m], w_recv.at[i, m], first + peer,
            )
            for m in range(groups)
        ]

    def each(copies, act):
        for copy in copies:
            getattr(copy, act)()

    def own_copies(act):
        for m in range(1, hops + 1):
            @pl.when(group + m < groups)
            def _():
                each(kv_copies(m * size), act)

            @pl.when(group >= m)
            def _():
                each(qd_copies(m * size), act)

        for j in range(1, size):
            @pl.when(rank + j < size)
            def _():
                each(kv_copies(j), act)

            @pl.when(rank >= j)
            def _():
                each(qd_copies(j), act)

    def pass_keys(m, act):
        for i in range(1, size):
            @pl.when(kv_goes(m, i))
            def _():
                each(kv_passes(m, i), act)

    def pass_queries(m, act):
        for i in range(1, size):
            @pl.when(qd_goes(m, i))
            def _():
                each(qd_passes(m, i), act)

    def take_keys(m):
        @pl.when(group >= m)
        def _():
            each(kv_copies(m * size), "wait_recv")

    def take_queries(m):
        @pl.when(group + m < groups)
        def _():
            each(qd_copies(m * size), "wait_recv")

    def ab_copy(j):
        return pltpu.make_async_remote_copy(
            src_ref=ab_buf.at[rank],
            dst_ref=ab_buf.at[rank],
            send_sem=ab_send.at[j - 1],
            recv_sem=ab_recv.at[j - 1],
            device_id={"seq": first + lax.rem(rank + j, size)},
            device_id_type=MESH,
        )

    def carry_copy():
        return pltpu.make_async_remote_copy(
            src_ref=carry_out,
            dst_ref=carry_in,
            send_sem=c_send,
            recv_sem=c_recv,
            device_id={"seq": lax.rem(me + n - size, n)},
            device_id_type=MESH,
        )

    own_copies("start")
    for m in range(1, groups):
        w_copy(m).start()

    row_ids = lax.broadcasted_iota(jnp.int32, (total, total), 0)
    col_ids = lax.broadcasted_iota(jnp.int32, (total, total), 1)
    shift = BLOCK.bit_length() - 1
    same = lax.shift_right_logical(row_ids, shift) == lax.shift_right_logical(col_ids, shift)
    eye = row_ids == col_ids
    causal = same & (row_ids >= col_ids)
    strict = same & (row_ids > col_ids)

    def to_column(row):
        return row_sum(jnp.where(eye, row, 0.0))

    def to_row(column):
        return column_sum(jnp.where(eye, column, 0.0))

    def flat_row(ref):
        return jnp.concatenate([ref[h : h + 1, :] for h in range(heads)], axis=1)

    decay_row = flat_row(decay_ref)
    decay_col = to_column(decay_row)
    beta = to_column(flat_row(beta_ref))
    summed = row_sum(jnp.where(causal, decay_row, 0.0))
    summed_row = column_sum(jnp.where(same & (row_ids <= col_ids), decay_col, 0.0))
    whole = row_sum(jnp.where(same, decay_row, 0.0))
    growth = jnp.exp(summed)
    tail = jnp.exp(row_sum(jnp.where(same & (row_ids < col_ids), decay_row, 0.0)))
    end_growth = jnp.exp(whole)
    raw_q = stack_heads(gq_ref[...], heads).astype(F32)
    raw_k = stack_heads(gk_ref[...], heads).astype(F32)
    values = stack_heads(gv_ref[...], heads).astype(F32)
    out_grad = stack_heads(gdo_ref[...], heads).astype(F32)
    inv_q = lax.rsqrt(row_sum(raw_q * raw_q) + EPS)
    inv_k = lax.rsqrt(row_sum(raw_k * raw_k) + EPS)
    scaling = depth ** (-0.5)
    unit_q = raw_q * inv_q * scaling
    unit_k = raw_k * inv_k
    fading = jnp.where(causal, jnp.exp(jnp.where(causal, summed - summed_row, 0.0)), 0.0)
    products = mm(jnp.concatenate([unit_k, unit_q], axis=0), unit_k, NT)
    key_products = products[:total]
    query_products = products[total:]
    strict_fading = jnp.where(strict, fading, 0.0)
    faded_keys = strict_fading * key_products
    lower = beta * faded_keys
    solved = jnp.where(eye, 1.0, 0.0) - lower
    powered = mm(lower, lower)
    for step in range(BLOCK.bit_length() - 2):
        if step < BLOCK.bit_length() - 3:
            both = mm(jnp.concatenate([solved, powered], axis=0), powered)
            solved = solved + both[:total]
            powered = both[total:]
        else:
            solved = solved + mm(solved, powered)
    early = group < groups - 2

    if hops:
        @pl.when(early)
        def _():
            take_keys(1)
            pass_keys(1, "start")

    attention = fading * query_products
    widened = mm(solved, (beta * growth) * unit_k)
    pulled = mm(attention, out_grad, TN)
    tailing = tail * unit_k
    grown_q = growth * unit_q

    def part(matrix, h, b):
        start = h * rows + b * BLOCK
        return matrix[start : start + BLOCK]

    depth_eye = jnp.where(
        lax.broadcasted_iota(jnp.int32, (depth, depth), 0)
        == lax.broadcasted_iota(jnp.int32, (depth, depth), 1),
        1.0,
        0.0,
    )
    for h in range(heads):
        across = None
        for b in reversed(range(blocks)):
            wide = part(widened, h, b)
            right = jnp.concatenate([part(tailing, h, b), part(pulled, h, b)], axis=1)
            product = mm(wide, right, TN)
            carry_map = part(end_growth, h, b)[0:1, :] * depth_eye - product[:, :depth]
            local = mm(part(grown_q, h, b), part(out_grad, h, b), TN) - product[:, depth:]
            map_buf[h, b, :, :depth] = carry_map
            map_buf[h, b, :, depth:] = local
            if across is None:
                across, offset = carry_map, local
            else:
                joined = mm(carry_map, jnp.concatenate([across, offset], axis=1))
                across, offset = joined[:, :depth], joined[:, depth:] + local
        ab_buf[rank, h, :, :depth] = (across - depth_eye).astype(BF16)
        ab_buf[rank, h, :, depth:] = offset.astype(BF16)

    key_ids = lax.broadcasted_iota(jnp.int32, (rows, rows), 0)
    query_ids = lax.broadcasted_iota(jnp.int32, (rows, rows), 1)

    def pair_terms(keys, vals, queries, grads, lse, dots, mask):
        logits = dot(keys, queries, NT) * scaling
        shifted = logits - lse
        if mask is None:
            chances = jnp.exp(shifted)
        else:
            chances = jnp.where(mask, jnp.exp(jnp.where(mask, shifted, 0.0)), 0.0)
        grad_prob = dot(vals, grads, NT)
        return (chances * (grad_prob - dots)).astype(BF16), chances.astype(BF16)

    def cut(ref_value, h):
        return ref_value[:, h * depth : (h + 1) * depth]

    for h in range(heads):
        grad_logit, weights = pair_terms(
            cut(k_ref, h), cut(v_ref, h), cut(q_ref, h), cut(dout_ref, h),
            stat_own[h : h + 1, :], stat_own[heads + h : heads + h + 1, :], query_ids >= key_ids,
        )
        cols = slice(h * depth, (h + 1) * depth)
        dq_acc[:, cols] = dot(grad_logit, cut(k_ref, h), TN)
        dkv_acc[:, cols] = dot(grad_logit, cut(q_ref, h))
        dkv_acc[:, columns + h * depth : columns + (h + 1) * depth] = dot(weights, cut(dout_ref, h))

    for j in range(1, size):
        ab_copy(j).start()
    for m in range(1, hops + 1):
        if m > 1:
            take_keys(m)
            pass_keys(m, "start")
        else:
            @pl.when(jnp.logical_not(early))
            def _():
                take_keys(1)
                pass_keys(1, "start")

        take_queries(m)
        pass_queries(m, "start")
    for m in range(1, groups):
        w_copy(m).wait_recv()
    for i in range(1, size):
        each(w_passes(i), "start")

    def attend(distances, keys_here, queries_here):
        for j in distances:
            mask = query_ids + j * rows - key_ids < WINDOW if (j + 1) * rows > WINDOW else None

            @pl.when(keys_here(j))
            def _():
                if j % size:
                    each(kv_copies(j), "wait_recv")
                for h in range(heads):
                    cols = slice(h * depth, (h + 1) * depth)
                    keys = kv_buf[j - 1, 0, :, cols]
                    grad_logit, _ = pair_terms(
                        keys, kv_buf[j - 1, 1, :, cols], cut(q_ref, h), cut(dout_ref, h),
                        stat_own[h : h + 1, :], stat_own[heads + h : heads + h + 1, :], mask,
                    )
                    dq_acc[:, cols] += dot(grad_logit, keys, TN)

            @pl.when(queries_here(j))
            def _():
                if j % size:
                    each(qd_copies(j), "wait_recv")
                for h in range(heads):
                    cols = slice(h * depth, (h + 1) * depth)
                    queries = qd_buf[j - 1, 0, :, cols]
                    grads = qd_buf[j - 1, 1, :, cols]
                    grad_logit, weights = pair_terms(
                        cut(k_ref, h), cut(v_ref, h), queries, grads,
                        stat_buf[j - 1, h : h + 1, :],
                        stat_buf[j - 1, heads + h : heads + h + 1, :], mask,
                    )
                    dkv_acc[:, cols] += dot(grad_logit, queries)
                    dkv_acc[:, columns + h * depth : columns + (h + 1) * depth] += dot(
                        weights, grads
                    )

    attend(range(1, size), lambda j: rank >= j, lambda j: rank + j < size)
    attend(
        range(size, hops * size + 1, size), lambda j: me >= j, lambda j: me + j < n
    )

    pairs = [(h, b) for h in range(heads) for b in range(blocks)]

    def by_parts(make):
        return jnp.concatenate([make(h, b) for h, b in pairs], axis=0)

    reads = [
        mm(jnp.concatenate([part(unit_k, h, b), part(unit_q, h, b)], axis=0), states_ref[b, h])
        for h, b in pairs
    ]
    key_reads = jnp.concatenate([item[:BLOCK] for item in reads], axis=0)
    query_reads = jnp.concatenate([item[BLOCK:] for item in reads], axis=0)
    remainder = values - growth * key_reads
    fresh = mm(solved, beta * remainder)
    faded_grad = fading * mm(out_grad, fresh, NT)
    out_back = by_parts(lambda h, b: mm_once(part(out_grad, h, b), states_ref[b, h], NT))
    unit_q_grad = growth * out_back + mm_once(faded_grad, unit_k)
    faded_back = mm_once(faded_grad, unit_q, TN)

    for j in range(1, size):
        ab_copy(j).wait_recv()
    inside = []
    for h in range(heads):
        joined = jnp.concatenate([depth_eye, jnp.zeros((depth, depth), F32)], axis=1)
        suffix = joined
        for r in reversed(range(size)):
            suffix = jnp.where(rank == r, joined, suffix)
            change = ab_buf[r, h, :, :depth]
            later = joined
            high, low = split(later)
            joined = later + (dot(change, high) + dot(change, low))
            joined = jnp.concatenate(
                [joined[:, :depth], joined[:, depth:] + ab_buf[r, h, :, depth:].astype(F32)], axis=1
            )
        inside.append((joined, suffix))

    @pl.when(group == groups - 1)
    def _():
        carry_in[...] = jnp.zeros_like(carry_in)

    if groups > 1:
        @pl.when(group < groups - 1)
        def _():
            carry_copy().wait_recv()

    for h in range(heads):
        joined, _ = inside[h]
        high, low = split(joined[:, :depth])
        state = carry_in[h]
        carry_out[h] = (dot(high, state) + dot(low, state) + joined[:, depth:]).astype(BF16)
    if groups > 1:
        @pl.when(group > 0)
        def _():
            carry_copy().start()

    later = {}
    for h in range(heads):
        _, suffix = inside[h]
        high, low = split(suffix[:, :depth])
        state = carry_in[h]
        adjoint = dot(high, state) + dot(low, state) + suffix[:, depth:]
        for b in reversed(range(blocks)):
            later[h, b] = adjoint
            if b > 0:
                adjoint = mm(map_buf[h, b, :, :depth], adjoint) + map_buf[h, b, :, depth:]
    fresh_grad = pulled + by_parts(lambda h, b: mm(part(tailing, h, b), later[h, b]))
    solved_grad = mm(solved, fresh_grad, TN)
    lower_grad = -mm(solved_grad, fresh, NT)
    key_products_grad = beta * strict_fading * lower_grad
    value_grad = beta * solved_grad
    value_back = by_parts(lambda h, b: mm_once(part(value_grad, h, b), states_ref[b, h], NT))
    fresh_back = tail * by_parts(lambda h, b: mm(part(fresh, h, b), later[h, b], NT))
    unit_k_grad = (
        fresh_back
        - growth * value_back
        + faded_back
        + mm_once(key_products_grad, unit_k)
        + mm_once(key_products_grad, unit_k, TN)
    )
    q_grad = scaling * inv_q * (unit_q_grad - raw_q * (inv_q * inv_q * row_sum(unit_q_grad * raw_q)))
    k_grad = inv_k * (unit_k_grad - raw_k * (inv_k * inv_k * row_sum(unit_k_grad * raw_k)))
    for h in range(heads):
        cols = slice(h * depth, (h + 1) * depth)
        own = slice(h * rows, (h + 1) * rows)
        gdq_out[:, cols] = q_grad[own].astype(BF16)
        gdk_out[:, cols] = k_grad[own].astype(BF16)
        gdv_out[:, cols] = value_grad[own].astype(BF16)
    beta_grad = row_sum(solved_grad * remainder) + row_sum(lower_grad * faded_keys)
    exponent = faded_grad * query_products + key_products_grad * key_products
    tail_grad = row_sum(unit_k * fresh_back)
    growth_grad = row_sum(out_grad * query_reads) - row_sum(value_grad * key_reads)
    summed_grad = (
        row_sum(exponent) - to_column(column_sum(exponent)) - tail_grad + growth * growth_grad
    )
    end_grad = end_growth * by_parts(
        lambda h, b: jnp.broadcast_to(
            column_sum(row_sum(later[h, b] * states_ref[b, h])), (BLOCK, 1)
        )
    )
    decay_grad = (
        column_sum(jnp.where(causal, summed_grad, 0.0))
        + column_sum(jnp.where(same, tail_grad, 0.0))
        + to_row(end_grad)
    )
    beta_row = to_row(beta_grad)
    for h in range(heads):
        own = slice(h * rows, (h + 1) * rows)
        gdecay_out[h : h + 1, :] = decay_grad[:, own]
        gbeta_out[h : h + 1, :] = beta_row[:, own]

    attend(
        [j for j in range(1, min(reach, n - 1) + 1) if j % size],
        lambda j: (me >= j) & (rank < j),
        lambda j: (me + j < n) & (rank + j >= size),
    )

    dq_out[...] = (dq_acc[...] * scaling).astype(BF16)
    both_grads = jnp.concatenate(
        [(dkv_acc[:, :columns] * scaling).astype(BF16), dkv_acc[:, columns:].astype(BF16)], axis=1
    )
    w_all[me] = w_ref[...]
    for i in range(1, size):
        each(w_passes(i), "wait_recv")
    out_rows = dx_out.shape[0]
    pieces_each = out_rows // w_rows

    def dx_rows(owner):
        piece = w_all[pl.ds(owner * pieces_each, pieces_each)].reshape(out_rows, 2 * columns)
        return dot(piece, both_grads, NT)

    def dx_copy(j):
        return pltpu.make_async_remote_copy(
            src_ref=dx_send.at[j - 1],
            dst_ref=dx_recv.at[j - 1],
            send_sem=x_send.at[j - 1],
            recv_sem=x_recv.at[j - 1],
            device_id={"head": lax.rem(my_head + j, head_n)},
            device_id_type=MESH,
        )

    for j in range(1, head_n):
        dx_send[j - 1] = dx_rows(lax.rem(my_head + j, head_n))
        dx_copy(j).start()
    result = dx_rows(my_head)
    for j in range(1, head_n):
        dx_copy(j).wait_recv()
        result = result + dx_recv[j - 1]
    dx_out[...] = result.astype(BF16)

    own_copies("wait_send")
    for m in range(1, hops + 1):
        pass_keys(m, "wait_send")
        pass_queries(m, "wait_send")
    for m in range(1, groups):
        w_copy(m).wait_send()
    for i in range(1, size):
        each(w_passes(i), "wait_send")
    for j in range(1, size):
        ab_copy(j).wait_send()
    if groups > 1:
        @pl.when(group > 0)
        def _():
            carry_copy().wait_send()

    for j in range(1, head_n):
        dx_copy(j).wait_send()


def hand_over(*refs):
    half = len(refs) // 2
    for source, target in zip(refs[:half], refs[half:]):
        target[...] = source[...]


def per_device(n, head_n, *args):
    attn_q, attn_lse, w_kv, states = args[0], args[5], args[6], args[13]
    rows, columns = attn_q.shape
    heads = attn_lse.shape[0]
    depth = columns // heads
    reach = min(WINDOW // rows, n - 1)
    size = group_size(n, WINDOW // rows)
    blocks = states.shape[0]
    groups = n // size
    hops = max(min(reach // size, groups - 1), 1)
    w_rows = w_kv.shape[0]
    out_rows = n * w_rows // head_n
    args = list(args)
    args[6] = w_kv.reshape(w_rows, 2 * columns)
    dma = pltpu.SemaphoreType.DMA
    vmem = pl.BlockSpec(memory_space=pltpu.VMEM)
    others = max(head_n - 1, 1)
    results = pl.pallas_call(
        functools.partial(kernel, n, head_n),
        out_shape=(
            jax.ShapeDtypeStruct((rows, columns), BF16),
            jax.ShapeDtypeStruct((out_rows, rows), BF16),
            jax.ShapeDtypeStruct((rows, columns), BF16),
            jax.ShapeDtypeStruct((rows, columns), BF16),
            jax.ShapeDtypeStruct((rows, columns), BF16),
            jax.ShapeDtypeStruct((heads, rows), F32),
            jax.ShapeDtypeStruct((heads, rows), F32),
        ),
        in_specs=[vmem] * len(args),
        out_specs=(vmem,) * 7,
        scratch_shapes=[
            pltpu.VMEM((reach, 2, rows, columns), BF16),
            pltpu.VMEM((reach, 2, rows, columns), BF16),
            pltpu.VMEM((2 * heads, rows), F32),
            pltpu.VMEM((reach, 2 * heads, rows), F32),
            pltpu.VMEM((n, w_rows, 2 * columns), BF16),
            pltpu.VMEM((size, heads, depth, 2 * depth), BF16),
            pltpu.VMEM((heads, depth, depth), BF16),
            pltpu.VMEM((heads, depth, depth), BF16),
            pltpu.VMEM((others, out_rows, rows), F32),
            pltpu.VMEM((others, out_rows, rows), F32),
            pltpu.VMEM((rows, columns), F32),
            pltpu.VMEM((rows, 2 * columns), F32),
            pltpu.VMEM((heads, blocks, depth, 2 * depth), F32),
            dma((reach, 2)), dma((reach, 2)),
            dma((reach, 2)), dma((reach, 2)),
            dma((reach,)), dma((reach,)),
            dma((groups,)), dma((size, groups)),
            dma((hops, size, 2)), dma((hops, size, 2)), dma((hops, size)), dma((size, groups)),
            dma((size,)), dma((size,)),
            dma, dma,
            dma((others,)), dma((others,)),
        ],
        compiler_params=pltpu.CompilerParams(
            collective_id=0, has_side_effects=True, vmem_limit_bytes=60000000
        ),
        name="layer_backward",
    )(*args)
    return pl.pallas_call(
        hand_over,
        out_shape=[jax.ShapeDtypeStruct(item.shape, item.dtype) for item in results],
        in_specs=[vmem] * len(results),
        out_specs=[vmem] * len(results),
        name="hand_over",
    )(*results)


def solution(mesh):
    rows = P("seq", "head")
    gates = P("head", "seq")
    return jax.shard_map(
        functools.partial(per_device, mesh.shape["seq"], mesh.shape["head"]),
        mesh=mesh,
        in_specs=(
            rows, rows, rows, rows, rows, gates, P("seq", None, "head"),
            rows, rows, rows, rows, gates, gates, P("seq", "head", None, None),
        ),
        out_specs=(rows, gates, rows, rows, rows, gates, gates),
        check_vma=False,
    )
```

profile of v0, /device:TPU:13, one launch (start us, length us, event | category | flops | bytes accessed | tf_op | source)
XLA Modules:
  0.0 48.7 jit_solution(16634816006735587728)
XLA Ops:
  0.6 1.4 %copy.21 = bf16[4,8,2,256]{3,1,2,0:T(8,128)(2,1)} copy(bf16[4,8,2,256]{3,2,1,0:T(2,128)(2,1)} %bitcast.3) | data formatting | bytes 65536
  2.0 45.0 %layer_backward.1 = (bf16[128,256]{1,0:T(8,128)(2,1)}, bf16[256,128]{1,0:T(8,128)(2,1)}, bf16[128,256]{1,0:T(8,128)(2,1)}, bf16[128,256]{1,0:T(8,128)(2,1)}, bf1...) custom-call(bf16[128,256]{1,0:T(8,128)(2,1)} %q_ref.1, bf16[128,256]{1,0:T(8,128)(2,1)} %k_ref.1, ...), custom_call_target="tpu_custom_call" | custom-call | tf_op jit(solution)/shard_map/layer_backward/pallas_call | solution.py:636
  47.0 1.7 %hand_over.1 = (bf16[128,256]{1,0:T(8,128)(2,1)}, bf16[256,128]{1,0:T(8,128)(2,1)}, bf16[128,256]{1,0:T(8,128)(2,1)}, bf16[128,256]{1,0:T(8,128)(2,1)}, bf16[128...) custom-call(bf16[128,256]{1,0:T(8,128)(2,1)} %get-tuple-element.14.refs_0_, ...), custom_call_target="tpu_custom_call" | custom-call | tf_op jit(solution)/shard_map/hand_over/pallas_call | solution.py:677
where the time goes:
time: 49 us; the launch traced here: 48.7 us
  Pallas kernels  46.7 us (95%)
  local copies, waits for them, and re-layouts  1.38 us (3%)
  between operations  0.64 us (1%)
    pallas_call x1, Pallas kernels, per_device(): pl.pallas_call(functools.partial(kernel, n, head_n), out_shape=(jax.Shape...  45 us
    pallas_call x1, Pallas kernels, per_device(): pl.pallas_call(hand_over, out_shape=[jax.ShapeDtypeStruct(item.shape, ite...  1.7 us
    unnamed x1, local copies, waits for them, and re-layouts  1.38 us

commit v1 on v0

v1 whole, which is shorter than its diff:
```python
import functools
import jax
import jax.numpy as jnp
from jax import lax
from jax.experimental import pallas as pl
from jax.experimental.pallas import tpu as pltpu
from jax.sharding import PartitionSpec as P

BLOCK = 64
WINDOW = 1024
EPS = 1e-06
MESH = pl.DeviceIdType.MESH
F32 = jnp.float32
BF16 = jnp.bfloat16

NN = (((1,), (0,)), ((), ()))
NT = (((1,), (1,)), ((), ()))
TN = (((0,), (0,)), ((), ()))


def dot(left, right, dims=NN):
    return lax.dot_general(left, right, dims, preferred_element_type=F32)


def split(matrix):
    high = matrix.astype(BF16)
    return high, (matrix - high.astype(F32)).astype(BF16)


def mm(left, right, dims=NN):
    left_high, left_low = split(left)
    right_high, right_low = split(right)
    return dot(left_high, right_high, dims) + (
        dot(left_high, right_low, dims) + dot(left_low, right_high, dims)
    )


def mm_once(left, right, dims=NN):
    return dot(left.astype(BF16), right.astype(BF16), dims)


def mm_full(left, right, dims=NN):
    return lax.dot_general(
        left, right, dims, precision=lax.Precision.HIGHEST, preferred_element_type=F32
    )


def row_sum(matrix):
    return jnp.sum(matrix, axis=1, keepdims=True)


def column_sum(matrix):
    return jnp.sum(matrix, axis=0, keepdims=True)


def stack_heads(matrix, heads):
    depth = matrix.shape[1] // heads
    return jnp.concatenate([matrix[:, h * depth : (h + 1) * depth] for h in range(heads)], axis=0)


def kernel(
    n,
    head_n,
    q_ref, k_ref, v_ref, out_ref, dout_ref, lse_ref, w_ref,
    gq_ref, gk_ref, gv_ref, gdo_ref, decay_ref, beta_ref, states_ref,
    dq_out, dx_out, gdq_out, gdk_out, gdv_out, gdecay_out, gbeta_out,
    kv_buf, qd_buf, stat_buf, stat_own, w_flat, w_all, ab_send_buf, ab_buf,
    map_hi, map_lo, map_add, carry_in, carry_out, adj_out, adj_in,
    grad_out, grad_in, dx_send, dx_recv, dq_acc, dk_acc, dv_acc, map_buf,
    a_send, a_recv, z_send, z_recv, p_send, p_recv,
    w_send, w_recv, w_pass, ab_send, ab_recv, c_send, c_recv, j_send, j_recv,
    t_send, t_recv, x_send, x_recv,
):
    me = lax.axis_index("seq")
    my_head = lax.axis_index("head")
    rows, columns = q_ref.shape
    heads = lse_ref.shape[0]
    depth = columns // heads
    blocks = rows // BLOCK
    total = heads * rows
    size = 2 * heads
    groups = n // size
    steps = WINDOW // (size * rows)
    reach = 2 * steps
    rank = lax.rem(me, size)
    group = lax.div(me, size)
    first = group * size
    core = lax.rem(my_head, 2)
    pair = my_head - core
    partner = pair + 1 - core
    half = lax.div(rank, heads)
    place = lax.rem(rank, heads)
    place_rows = pl.ds(pl.multiple_of(place * rows, rows), rows)
    composer = half == core
    scaling = depth ** (-0.5)

    barrier = pltpu.get_barrier_semaphore()

    def greet(device):
        pl.semaphore_signal(barrier, inc=1, device_id=device, device_id_type=MESH)

    for j in range(1, size):
        peer = first + lax.rem(rank + j, size)
        greet({"seq": peer, "head": my_head})
        greet({"seq": peer, "head": partner})
    for m in range(1, groups):
        greet({"seq": lax.rem(me + m * size, n), "head": my_head})
    for j in range(1, head_n):
        greet({"seq": me, "head": lax.rem(my_head + j, head_n)})
    greeted = 2 * (size - 1) + groups - 1 + head_n - 1

    ones = jnp.ones((8, depth), F32)
    top = lax.broadcasted_iota(jnp.int32, (8, rows), 0) == 0
    for h in range(heads):
        cols = slice(h * depth, (h + 1) * depth)
        product = dout_ref[:, cols].astype(F32) * out_ref[:, cols].astype(F32)
        stat_own[h] = jnp.where(top, lse_ref[h : h + 1, :], mm_full(ones, product, NT))
    w_flat[:, :columns] = w_ref[:, 0, :]
    w_flat[:, columns:] = w_ref[:, 1, :]
    pl.semaphore_wait(barrier, greeted)

    def move(source, target, sent, received, seq, head):
        return pltpu.make_async_remote_copy(
            src_ref=source,
            dst_ref=target,
            send_sem=sent,
            recv_sem=received,
            device_id={"seq": seq, "head": head},
            device_id_type=MESH,
        )

    own_kv = 1 - core
    own_qd = core

    def spread_refs(h, kind):
        cols = slice(h * depth, (h + 1) * depth)
        if kind == 4:
            return stat_own.at[h], stat_buf.at[half, place]
        source = (k_ref, v_ref, q_ref, dout_ref)[kind].at[:, cols]
        if kind < 2:
            return source, kv_buf.at[1 - half, kind, place_rows, :]
        return source, qd_buf.at[half, kind - 2, place_rows, :]

    def spread(h, kind):
        source, target = spread_refs(h, kind)
        return move(
            source, target, a_send.at[h, kind], a_recv.at[place, kind],
            first + heads * core + h, pair + half,
        )

    def spread_here(h, kind):
        source, target = spread_refs(h, kind)
        return pltpu.make_async_copy(source, target, a_recv.at[place, kind])

    def spread_in(block, kind):
        part_rows = slice(block * rows, (block + 1) * rows)
        if kind == 4:
            target = stat_buf.at[own_qd, block]
        elif kind < 2:
            target = kv_buf.at[own_kv, kind, part_rows, :]
        else:
            target = qd_buf.at[own_qd, kind - 2, part_rows, :]
        return move(
            target, target, a_send.at[0, kind], a_recv.at[block, kind], me, partner
        )

    def start_spread(kinds):
        for kind in kinds:
            for h in range(heads):
                @pl.when(heads * core + h == rank)
                def _():
                    spread_here(h, kind).start()

                @pl.when(heads * core + h != rank)
                def _():
                    spread(h, kind).start()

    def take_spread(kinds):
        for kind in kinds:
            for block in range(heads):
                spread_in(block, kind).wait_recv()

    def chunk(kind, index):
        if kind == 4:
            return stat_buf.at[index]
        if kind < 2:
            return kv_buf.at[index, kind]
        return qd_buf.at[index, kind - 2]

    def slot(kind, m, lane):
        return 2 * m + 1 - lane if kind < 2 else 2 * m + lane

    def hop(kind, m):
        return move(
            chunk(kind, slot(kind, m - 1, core)), chunk(kind, slot(kind, m, core)),
            z_send.at[m - 1, kind], z_recv.at[m - 1, kind],
            lax.rem(me + (size if kind < 2 else n - size), n), my_head,
        )

    def hop_goes(kind, m):
        if kind < 2:
            return (group >= m - 1) & (group + 1 < groups)
        return (group + m - 1 < groups) & (group >= 1)

    def there(kind, m):
        return group >= m if kind < 2 else group + m < groups

    def share(kind, m):
        refs = chunk(kind, slot(kind, m, core))
        return move(refs, refs, p_send.at[m, kind], p_recv.at[m, kind], me, partner)

    def share_in(kind, m):
        refs = chunk(kind, slot(kind, m, 1 - core))
        return move(refs, refs, p_send.at[m, kind], p_recv.at[m, kind], me, partner)

    def share_goes(kind, m):
        near, far = (0, 1) if kind < 2 else (1, 0)
        needed = there(kind, m)
        if m == 0:
            needed = needed & (core == near)
        if m == steps:
            needed = needed & (core == far)
        return needed

    def share_comes(kind, m):
        near, far = (1, 0) if kind < 2 else (0, 1)
        needed = there(kind, m)
        if m == 0:
            needed = needed & (core == near)
        if m == steps:
            needed = needed & (core == far)
        return needed

    KEYS = (0, 1)
    QUERIES = (2, 3, 4)

    def act_if(condition, copy, act):
        @pl.when(condition)
        def _():
            getattr(copy, act)()

    def send_on(kinds, m):
        for kind in kinds:
            if m < steps:
                act_if(hop_goes(kind, m + 1), hop(kind, m + 1), "start")
        for kind in kinds:
            act_if(share_goes(kind, m), share(kind, m), "start")

    def arrive(kinds, m):
        for kind in kinds:
            act_if(there(kind, m), hop(kind, m), "wait_recv")
            if m < steps:
                act_if(hop_goes(kind, m + 1), hop(kind, m + 1), "start")
            act_if(share_goes(kind, m), share(kind, m), "start")

    w_rows = w_ref.shape[0]

    def w_copy(m):
        return move(
            w_flat, w_all.at[me], w_send.at[m - 1], w_recv.at[0, m],
            lax.rem(me + m * size, n), my_head,
        )

    def w_passes(i):
        peer = first + lax.rem(rank + i, size)
        return [
            move(
                w_flat if m == 0 else w_all.at[lax.rem(me + n - m * size, n)],
                w_all.at[lax.rem(me + n - m * size, n)],
                w_pass.at[i, m], w_recv.at[i, m], peer, my_head,
            )
            for m in range(groups)
        ]

    def each(copies, act):
        for copy in copies:
            getattr(copy, act)()

    def ab_copy(h):
        return move(
            ab_send_buf.at[h], ab_buf.at[rank], ab_send.at[h], ab_recv.at[rank],
            first + heads * core + h, my_head,
        )

    def ab_in(j):
        source = lax.rem(rank + j, size)
        return move(
            ab_buf.at[source], ab_buf.at[source], ab_send.at[0], ab_recv.at[source], me, partner
        )

    def carry_copy():
        return move(carry_out, carry_in, c_send, c_recv, lax.rem(me + n - size, n), my_head)

    def adj_copy(j):
        target = lax.rem(rank + j, size)
        return move(
            adj_out.at[target], adj_in.at[place], j_send.at[j - 1], j_recv.at[place],
            first + target, my_head,
        )

    def adj_arrival(h):
        return move(adj_in.at[h], adj_in.at[h], j_send.at[0], j_recv.at[h], me, partner)

    def back_rank(block):
        return core * heads + block

    def back_copy(block, item):
        return move(
            grad_out.at[item, block], grad_in.at[place, item],
            t_send.at[block, item], t_recv.at[place, item],
            first + back_rank(block), pair + half,
        )

    def back_here(block, item):
        return pltpu.make_async_copy(
            grad_out.at[item, block], grad_in.at[place, item], t_recv.at[place, item]
        )

    def back_in(h, item):
        return move(
            grad_in.at[h, item], grad_in.at[h, item],
            t_send.at[0, item], t_recv.at[h, item], me, partner,
        )

    def start_back(items):
        for item in items:
            for block in range(heads):
                act_if(back_rank(block) == rank, back_here(block, item), "start")
                act_if(back_rank(block) != rank, back_copy(block, item), "start")

    start_spread(KEYS + QUERIES)
    for m in range(1, groups):
        w_copy(m).start()

    row_ids = lax.broadcasted_iota(jnp.int32, (total, total), 0)
    col_ids = lax.broadcasted_iota(jnp.int32, (total, total), 1)
    shift = BLOCK.bit_length() - 1
    same = lax.shift_right_logical(row_ids, shift) == lax.shift_right_logical(col_ids, shift)
    eye = row_ids == col_ids
    causal = same & (row_ids >= col_ids)
    strict = same & (row_ids > col_ids)

    def to_column(row):
        return row_sum(jnp.where(eye, row, 0.0))

    def to_row(column):
        return column_sum(jnp.where(eye, column, 0.0))

    def flat_row(ref):
        return jnp.concatenate([ref[h : h + 1, :] for h in range(heads)], axis=1)

    decay_row = flat_row(decay_ref)
    decay_col = to_column(decay_row)
    beta = to_column(flat_row(beta_ref))
    summed = row_sum(jnp.where(causal, decay_row, 0.0))
    summed_row = column_sum(jnp.where(same & (row_ids <= col_ids), decay_col, 0.0))
    whole = row_sum(jnp.where(same, decay_row, 0.0))
    growth = jnp.exp(summed)
    tail = jnp.exp(row_sum(jnp.where(same & (row_ids < col_ids), decay_row, 0.0)))
    end_growth = jnp.exp(whole)
    raw_q = stack_heads(gq_ref[...], heads).astype(F32)
    raw_k = stack_heads(gk_ref[...], heads).astype(F32)
    values = stack_heads(gv_ref[...], heads).astype(F32)
    out_grad = stack_heads(gdo_ref[...], heads).astype(F32)
    inv_q = lax.rsqrt(row_sum(raw_q * raw_q) + EPS)
    inv_k = lax.rsqrt(row_sum(raw_k * raw_k) + EPS)
    unit_q = raw_q * inv_q * scaling
    unit_k = raw_k * inv_k
    fading = jnp.where(causal, jnp.exp(jnp.where(causal, summed - summed_row, 0.0)), 0.0)
    products = mm(jnp.concatenate([unit_k, unit_q], axis=0), unit_k, NT)
    key_products = products[:total]
    query_products = products[total:]
    strict_fading = jnp.where(strict, fading, 0.0)
    faded_keys = strict_fading * key_products
    lower = beta * faded_keys
    solved = jnp.where(eye, 1.0, 0.0) - lower
    powered = mm(lower, lower)
    for step in range(BLOCK.bit_length() - 2):
        if step < BLOCK.bit_length() - 3:
            both = mm(jnp.concatenate([solved, powered], axis=0), powered)
            solved = solved + both[:total]
            powered = both[total:]
        else:
            solved = solved + mm(solved, powered)
    attention = fading * query_products
    widened = mm(solved, (beta * growth) * unit_k)
    pulled = mm(attention, out_grad, TN)
    tailing = tail * unit_k
    grown_q = growth * unit_q

    def part(matrix, h, b):
        start = h * rows + b * BLOCK
        return matrix[start : start + BLOCK]

    depth_eye = jnp.where(
        lax.broadcasted_iota(jnp.int32, (depth, depth), 0)
        == lax.broadcasted_iota(jnp.int32, (depth, depth), 1),
        1.0,
        0.0,
    )
    for h in range(heads):
        across = None
        for b in reversed(range(blocks)):
            wide = part(widened, h, b)
            right = jnp.concatenate([part(tailing, h, b), part(pulled, h, b)], axis=1)
            product = mm(wide, right, TN)
            carry_map = part(end_growth, h, b)[0:1, :] * depth_eye - product[:, :depth]
            local = mm(part(grown_q, h, b), part(out_grad, h, b), TN) - product[:, depth:]
            map_buf[h, b, :, :depth] = carry_map
            map_buf[h, b, :, depth:] = local
            if across is None:
                across, offset = carry_map, local
            else:
                joined = mm(carry_map, jnp.concatenate([across, offset], axis=1))
                across, offset = joined[:, :depth], joined[:, depth:] + local
        change = jnp.concatenate([across - depth_eye, offset], axis=1).astype(BF16)
        ab_send_buf[h] = change

        @pl.when(heads * core + h == rank)
        def _():
            ab_buf[rank] = change

        act_if(heads * core + h != rank, ab_copy(h), "start")

    take_spread(KEYS)
    send_on(KEYS, 0)
    take_spread(QUERIES)
    send_on(QUERIES, 0)

    key_ids = row_ids
    query_ids = col_ids

    def stat_row(index, which):
        return jnp.concatenate(
            [stat_buf[index, block, which : which + 1, :] for block in range(heads)], axis=1
        )

    def terms(logits, grad_prob, lse, dots, mask):
        shifted = logits * scaling - lse
        if mask is None:
            chances = jnp.exp(shifted)
        else:
            chances = jnp.where(mask, jnp.exp(jnp.where(mask, shifted, 0.0)), 0.0)
        return (chances * (grad_prob - dots)).astype(BF16), chances.astype(BF16)

    own_lse = stat_row(own_qd, 0)
    own_dots = stat_row(own_qd, 1)
    keys = kv_buf[own_kv, 0]
    queries = qd_buf[own_qd, 0]
    grads = qd_buf[own_qd, 1]
    grad_logit, weights = terms(
        dot(keys, queries, NT), dot(kv_buf[own_kv, 1], grads, NT),
        own_lse, own_dots, query_ids >= key_ids,
    )
    dq_acc[...] = dot(grad_logit, keys, TN)
    dk_acc[...] = dot(grad_logit, queries)
    dv_acc[...] = dot(weights, grads)
    lse_column = to_column(own_lse)
    dots_column = to_column(own_dots)

    def attend_keys(d):
        @pl.when(2 * group + core >= d)
        def _():
            keys = kv_buf[d + 1 - core, 0]
            grad_logit, _ = terms(
                dot(qd_buf[own_qd, 0], keys, NT),
                dot(qd_buf[own_qd, 1], kv_buf[d + 1 - core, 1], NT),
                lse_column, dots_column, row_ids < col_ids if d == reach else None,
            )
            dq_acc[...] += dot(grad_logit, keys)

    def attend_queries(d):
        @pl.when(2 * group + core + d < 2 * groups)
        def _():
            queries = qd_buf[d + core, 0]
            grads = qd_buf[d + core, 1]
            grad_logit, weights = terms(
                dot(kv_buf[own_kv, 0], queries, NT), dot(kv_buf[own_kv, 1], grads, NT),
                stat_row(d + core, 0), stat_row(d + core, 1),
                query_ids < key_ids if d == reach else None,
            )
            dk_acc[...] += dot(grad_logit, queries)
            dv_acc[...] += dot(weights, grads)

    def attend_shared(d):
        for lane in range(2):
            m = (d + 1 - lane) // 2
            for kind in KEYS:
                act_if(share_comes(kind, m) & (core == lane), share_in(kind, m), "wait_recv")
        attend_keys(d)
        for lane in range(2):
            m = (d + lane) // 2
            for kind in QUERIES:
                act_if(share_comes(kind, m) & (core == lane), share_in(kind, m), "wait_recv")
        attend_queries(d)

    pairs = [(h, b) for h in range(heads) for b in range(blocks)]

    def by_parts(make):
        return jnp.concatenate([make(h, b) for h, b in pairs], axis=0)

    reads = [
        mm(jnp.concatenate([part(unit_k, h, b), part(unit_q, h, b)], axis=0), states_ref[b, h])
        for h, b in pairs
    ]
    key_reads = jnp.concatenate([item[:BLOCK] for item in reads], axis=0)
    query_reads = jnp.concatenate([item[BLOCK:] for item in reads], axis=0)
    remainder = values - growth * key_reads
    fresh = mm(solved, beta * remainder)
    faded_grad = fading * mm(out_grad, fresh, NT)
    out_back = by_parts(lambda h, b: mm_once(part(out_grad, h, b), states_ref[b, h], NT))
    unit_q_grad = growth * out_back + mm_once(faded_grad, unit_k)
    faded_back = mm_once(faded_grad, unit_q, TN)

    for m in range(1, groups):
        w_copy(m).wait_recv()
    for i in range(1, size):
        each(w_passes(i), "start")

    @pl.when(composer)
    def _():
        joined = None
        for j in range(1, size):
            ab_in(j).wait_recv()
        for r in reversed(range(size)):
            change = ab_buf[r, :, :depth]
            local = ab_buf[r, :, depth:].astype(F32)
            if joined is None:
                joined = jnp.concatenate([change.astype(F32) + depth_eye, local], axis=1)
            else:
                high, low = split(joined)
                joined = joined + (dot(change, high) + dot(change, low))
                joined = jnp.concatenate([joined[:, :depth], joined[:, depth:] + local], axis=1)
            map_hi[r], map_lo[r] = split(joined[:, :depth])
            map_add[r] = joined[:, depth:]

    def carry_step(condition):
        @pl.when(composer & condition)
        def _():
            @pl.when(group == groups - 1)
            def _():
                carry_in[...] = jnp.zeros_like(carry_in)

            act_if(group < groups - 1, carry_copy(), "wait_recv")
            state = carry_in[...]

            def start_of(r):
                return (dot(map_hi[r], state) + dot(map_lo[r], state) + map_add[r]).astype(BF16)

            carry_out[...] = start_of(0)
            act_if(group > 0, carry_copy(), "start")
            for r in range(size - 1):
                adj_out[r] = start_of(r + 1)
            adj_out[size - 1] = state
            for j in range(1, size):
                adj_copy(j).start()
            adj_in[place] = adj_out[rank]

    last = groups - 1 - group
    carry_step(last == 0)
    arrive(KEYS, 1)
    arrive(QUERIES, 1)
    attend_keys(2)
    attend_queries(2)
    carry_step(last == 1)
    attend_shared(1)
    for m in range(2, steps + 1):
        arrive(KEYS, m)
        arrive(QUERIES, m)
    carry_step(last == 2)
    for d in range(3, reach + 1):
        if d % 2:
            attend_shared(d)
        else:
            attend_keys(d)
            attend_queries(d)

    def blocks_of(matrix):
        return matrix.astype(BF16).reshape(heads, rows, depth)

    grad_out[1] = blocks_of(dk_acc[...] * scaling)
    grad_out[2] = blocks_of(dv_acc[...])
    grad_out[0] = blocks_of(dq_acc[...] * scaling)
    start_back((1, 2, 0))
    carry_step(last >= 3)

    for h in range(heads):
        act_if(heads * core + h != rank, adj_arrival(h), "wait_recv")
    later = {}
    for h in range(heads):
        adjoint = adj_in[h].astype(F32)
        for b in reversed(range(blocks)):
            later[h, b] = adjoint
            if b > 0:
                adjoint = mm(map_buf[h, b, :, :depth], adjoint) + map_buf[h, b, :, depth:]
    fresh_grad = pulled + by_parts(lambda h, b: mm(part(tailing, h, b), later[h, b]))
    solved_grad = mm(solved, fresh_grad, TN)
    lower_grad = -mm(solved_grad, fresh, NT)
    key_products_grad = beta * strict_fading * lower_grad
    value_grad = beta * solved_grad
    value_back = by_parts(lambda h, b: mm_once(part(value_grad, h, b), states_ref[b, h], NT))
    fresh_back = tail * by_parts(lambda h, b: mm(part(fresh, h, b), later[h, b], NT))
    unit_k_grad = (
        fresh_back
        - growth * value_back
        + faded_back
        + mm_once(key_products_grad, unit_k)
        + mm_once(key_products_grad, unit_k, TN)
    )
    q_grad = scaling * inv_q * (unit_q_grad - raw_q * (inv_q * inv_q * row_sum(unit_q_grad * raw_q)))
    k_grad = inv_k * (unit_k_grad - raw_k * (inv_k * inv_k * row_sum(unit_k_grad * raw_k)))
    for h in range(heads):
        cols = slice(h * depth, (h + 1) * depth)
        own = slice(h * rows, (h + 1) * rows)
        gdq_out[:, cols] = q_grad[own].astype(BF16)
        gdk_out[:, cols] = k_grad[own].astype(BF16)
        gdv_out[:, cols] = value_grad[own].astype(BF16)
    beta_grad = row_sum(solved_grad * remainder) + row_sum(lower_grad * faded_keys)
    exponent = faded_grad * query_products + key_products_grad * key_products
    tail_grad = row_sum(unit_k * fresh_back)
    growth_grad = row_sum(out_grad * query_reads) - row_sum(value_grad * key_reads)
    summed_grad = (
        row_sum(exponent) - to_column(column_sum(exponent)) - tail_grad + growth * growth_grad
    )
    end_grad = end_growth * by_parts(
        lambda h, b: jnp.broadcast_to(
            column_sum(row_sum(later[h, b] * states_ref[b, h])), (BLOCK, 1)
        )
    )
    decay_grad = (
        column_sum(jnp.where(causal, summed_grad, 0.0))
        + column_sum(jnp.where(same, tail_grad, 0.0))
        + to_row(end_grad)
    )
    beta_row = to_row(beta_grad)
    for h in range(heads):
        own = slice(h * rows, (h + 1) * rows)
        gdecay_out[h : h + 1, :] = decay_grad[:, own]
        gbeta_out[h : h + 1, :] = beta_row[:, own]

    for item in (1, 2, 0):
        for h in range(heads):
            back_in(h, item).wait_recv()
    for h in range(heads):
        dq_out[:, h * depth : (h + 1) * depth] = grad_in[h, 0]
    both_grads = jnp.concatenate(
        [grad_in[h, item] for item in (1, 2) for h in range(heads)], axis=1
    )
    w_all[me] = w_flat[...]
    for i in range(1, size):
        each(w_passes(i), "wait_recv")
    out_rows = dx_out.shape[0]
    pieces_each = out_rows // w_rows

    def dx_rows(owner):
        piece = w_all[pl.ds(owner * pieces_each, pieces_each)].reshape(out_rows, 2 * columns)
        return dot(piece, both_grads, NT)

    def dx_copy(j):
        return move(
            dx_send.at[j - 1], dx_recv.at[j - 1], x_send.at[j - 1], x_recv.at[j - 1],
            me, lax.rem(my_head + j, head_n),
        )

    for j in range(1, head_n):
        dx_send[j - 1] = dx_rows(lax.rem(my_head + j, head_n))
        dx_copy(j).start()
    result = dx_rows(my_head)
    for j in range(1, head_n):
        dx_copy(j).wait_recv()
        result = result + dx_recv[j - 1]
    dx_out[...] = result.astype(BF16)

    for kind in KEYS + QUERIES:
        for h in range(heads):
            act_if(heads * core + h != rank, spread(h, kind), "wait_send")
        for m in range(steps + 1):
            if m:
                act_if(hop_goes(kind, m), hop(kind, m), "wait_send")
            act_if(share_goes(kind, m), share(kind, m), "wait_send")
    for m in range(1, groups):
        w_copy(m).wait_send()
    for i in range(1, size):
        each(w_passes(i), "wait_send")
    for h in range(heads):
        act_if(heads * core + h != rank, ab_copy(h), "wait_send")
    act_if(composer & (group > 0), carry_copy(), "wait_send")
    for j in range(1, size):
        act_if(composer, adj_copy(j), "wait_send")
    for item in range(3):
        for block in range(heads):
            act_if(back_rank(block) != rank, back_copy(block, item), "wait_send")
    for j in range(1, head_n):
        dx_copy(j).wait_send()


def hand_over(*refs):
    half = len(refs) // 2
    for source, target in zip(refs[:half], refs[half:]):
        target[...] = source[...]


def per_device(n, head_n, *args):
    attn_q, attn_lse, w_kv, states = args[0], args[5], args[6], args[13]
    rows, columns = attn_q.shape
    heads = attn_lse.shape[0]
    depth = columns // heads
    size = 2 * heads
    steps = WINDOW // (size * rows)
    blocks = states.shape[0]
    groups = n // size
    assert head_n % 2 == 0 and n % size == 0 and WINDOW == steps * size * rows
    w_rows = w_kv.shape[0]
    out_rows = n * w_rows // head_n
    dma = pltpu.SemaphoreType.DMA
    vmem = pl.BlockSpec(memory_space=pltpu.VMEM)
    others = max(head_n - 1, 1)
    slots = 2 * (steps + 1)
    span = heads * rows
    results = pl.pallas_call(
        functools.partial(kernel, n, head_n),
        out_shape=(
            jax.ShapeDtypeStruct((rows, columns), BF16),
            jax.ShapeDtypeStruct((out_rows, rows), BF16),
            jax.ShapeDtypeStruct((rows, columns), BF16),
            jax.ShapeDtypeStruct((rows, columns), BF16),
            jax.ShapeDtypeStruct((rows, columns), BF16),
            jax.ShapeDtypeStruct((heads, rows), F32),
            jax.ShapeDtypeStruct((heads, rows), F32),
        ),
        in_specs=[vmem] * len(args),
        out_specs=(vmem,) * 7,
        scratch_shapes=[
            pltpu.VMEM((slots, 2, span, depth), BF16),
            pltpu.VMEM((slots, 2, span, depth), BF16),
            pltpu.VMEM((slots, heads, 8, rows), F32),
            pltpu.VMEM((heads, 8, rows), F32),
            pltpu.VMEM((w_rows, 2 * columns), BF16),
            pltpu.VMEM((n, w_rows, 2 * columns), BF16),
            pltpu.VMEM((heads, depth, 2 * depth), BF16),
            pltpu.VMEM((size, depth, 2 * depth), BF16),
            pltpu.VMEM((size, depth, depth), BF16),
            pltpu.VMEM((size, depth, depth), BF16),
            pltpu.VMEM((size, depth, depth), F32),
            pltpu.VMEM((depth, depth), BF16),
            pltpu.VMEM((depth, depth), BF16),
            pltpu.VMEM((size, depth, depth), BF16),
            pltpu.VMEM((heads, depth, depth), BF16),
            pltpu.VMEM((3, heads, rows, depth), BF16),
            pltpu.VMEM((heads, 3, rows, depth), BF16),
            pltpu.VMEM((others, out_rows, rows), F32),
            pltpu.VMEM((others, out_rows, rows), F32),
            pltpu.VMEM((span, depth), F32),
            pltpu.VMEM((span, depth), F32),
            pltpu.VMEM((span, depth), F32),
            pltpu.VMEM((heads, blocks, depth, 2 * depth), F32),
            dma((heads, 5)), dma((heads, 5)),
            dma((steps, 5)), dma((steps, 5)),
            dma((steps + 1, 5)), dma((steps + 1, 5)),
            dma((groups,)), dma((size, groups)), dma((size, groups)),
            dma((heads,)), dma((size,)),
            dma, dma,
            dma((size,)), dma((heads,)),
            dma((heads, 3)), dma((heads, 3)),
            dma((others,)), dma((others,)),
        ],
        compiler_params=pltpu.CompilerParams(
            collective_id=0, has_side_effects=True, vmem_limit_bytes=60000000
        ),
        name="layer_backward",
    )(*args)
    return pl.pallas_call(
        hand_over,
        out_shape=[jax.ShapeDtypeStruct(item.shape, item.dtype) for item in results],
        in_specs=[vmem] * len(results),
        out_specs=[vmem] * len(results),
        name="hand_over",
    )(*results)


def solution(mesh):
    rows = P("seq", "head")
    gates = P("head", "seq")
    return jax.shard_map(
        functools.partial(per_device, mesh.shape["seq"], mesh.shape["head"]),
        mesh=mesh,
        in_specs=(
            rows, rows, rows, rows, rows, gates, P("seq", None, "head"),
            rows, rows, rows, rows, gates, gates, P("seq", "head", None, None),
        ),
        out_specs=(rows, gates, rows, rows, rows, gates, gates),
        check_vma=False,
    )
```

time: 49 us -> 36.1 us (0.74)
  the two profiles are of different devices: /device:TPU:13 before, /device:TPU:0 now
where the time goes in v1:
time: 36.1 us; the launch traced here: 35.6 us
  Pallas kernels  35 us (97%)
  between operations  0.65 us (2%)
    pallas_call x1, Pallas kernels, per_device(): pl.pallas_call(functools.partial(kernel, n, head_n), out_shape=(jax.Shape...  33.3 us
    pallas_call x1, Pallas kernels, per_device(): pl.pallas_call(hand_over, out_shape=[jax.ShapeDtypeStruct(item.shape, ite...  1.7 us

profile of v1, /device:TPU:0, one launch (start us, length us, event | category | flops | bytes accessed | tf_op | source)
XLA Modules:
  0.0 35.6 jit_solution(14589836912673369031)
XLA Ops:
  0.6 33.3 %layer_backward.1 = (bf16[128,256]{1,0:T(8,128)(2,1)}, bf16[256,128]{1,0:T(8,128)(2,1)}, bf16[128,256]{1,0:T(8,128)(2,1)}, bf16[128,256]{1,0:T(8,128)(2,1)}, bf1...) custom-call(bf16[128,256]{1,0:T(8,128)(2,1)} %q_ref.1, bf16[128,256]{1,0:T(8,128)(2,1)} %k_ref.1, ...), custom_call_target="tpu_custom_call" | custom-call | tf_op jit(solution)/shard_map/layer_backward/pallas_call | solution.py:720
  33.9 1.7 %hand_over.1 = (bf16[128,256]{1,0:T(8,128)(2,1)}, bf16[256,128]{1,0:T(8,128)(2,1)}, bf16[128,256]{1,0:T(8,128)(2,1)}, bf16[128,256]{1,0:T(8,128)(2,1)}, bf16[128...) custom-call(bf16[128,256]{1,0:T(8,128)(2,1)} %get-tuple-element.14.refs_0_, ...), custom_call_target="tpu_custom_call" | custom-call | tf_op jit(solution)/shard_map/hand_over/pallas_call | solution.py:772

commit v2 on v1

--- a/solution.py
+++ b/solution.py
@@ -61,19 +61,21 @@
 def kernel(
     n,
     head_n,
-    q_ref, k_ref, v_ref, out_ref, dout_ref, lse_ref, w_ref,
+    q_hbm, k_hbm, v_hbm, out_hbm, dout_hbm, lse_hbm, w_hbm,
+    gq_hbm, gk_hbm, gv_hbm, gdo_hbm, decay_hbm, beta_hbm, states_hbm,
+    dq_out, dx_out, gdq_out, gdk_out, gdv_out, gdecay_out, gbeta_out,
+    out_ref, dout_ref, lse_ref, w_ref,
     gq_ref, gk_ref, gv_ref, gdo_ref, decay_ref, beta_ref, states_ref,
-    dq_out, dx_out, gdq_out, gdk_out, gdv_out, gdecay_out, gbeta_out,
-    kv_buf, qd_buf, stat_buf, stat_own, w_flat, w_all, ab_send_buf, ab_buf,
-    map_hi, map_lo, map_add, carry_in, carry_out, adj_out, adj_in,
+    kv_buf, qd_buf, stat_buf, stat_own, w_all, ab_send_buf, ab_buf,
+    map_hi, map_lo, map_add, whole_out, whole_in, carry_in, carry_out, adj_out, adj_in,
     grad_out, grad_in, dx_send, dx_recv, dq_acc, dk_acc, dv_acc, map_buf,
-    a_send, a_recv, z_send, z_recv, p_send, p_recv,
-    w_send, w_recv, w_pass, ab_send, ab_recv, c_send, c_recv, j_send, j_recv,
-    t_send, t_recv, x_send, x_recv,
+    sems, a_recv, z_send, z_recv, p_send, p_recv,
+    w_send, w_recv, w_pass, w_taken, ab_send, ab_recv, o_send, o_recv, c_send, c_recv, j_recv,
+    t_recv, x_recv,
 ):
     me = lax.axis_index("seq")
     my_head = lax.axis_index("head")
-    rows, columns = q_ref.shape
+    rows, columns = q_hbm.shape
     heads = lse_ref.shape[0]
     depth = columns // heads
     blocks = rows // BLOCK
@@ -109,15 +111,27 @@
         greet({"seq": me, "head": lax.rem(my_head + j, head_n)})
     greeted = 2 * (size - 1) + groups - 1 + head_n - 1
 
-    ones = jnp.ones((8, depth), F32)
-    top = lax.broadcasted_iota(jnp.int32, (8, rows), 0) == 0
-    for h in range(heads):
-        cols = slice(h * depth, (h + 1) * depth)
-        product = dout_ref[:, cols].astype(F32) * out_ref[:, cols].astype(F32)
-        stat_own[h] = jnp.where(top, lse_ref[h : h + 1, :], mm_full(ones, product, NT))
-    w_flat[:, :columns] = w_ref[:, 0, :]
-    w_flat[:, columns:] = w_ref[:, 1, :]
-    pl.semaphore_wait(barrier, greeted)
+    def load(source, target, index):
+        copy = pltpu.make_async_copy(source, target, sems.at[index])
+        copy.start()
+        return copy
+
+    gdn_loads = [
+        load(source, target, index)
+        for index, (source, target) in enumerate([
+            (decay_hbm, decay_ref), (beta_hbm, beta_ref), (gk_hbm, gk_ref), (gq_hbm, gq_ref),
+            (gv_hbm, gv_ref), (gdo_hbm, gdo_ref),
+        ])
+    ]
+    attention_loads = [
+        load(source, target, len(gdn_loads) + index)
+        for index, (source, target) in enumerate([
+            (lse_hbm, lse_ref), (dout_hbm, dout_ref), (out_hbm, out_ref), (w_hbm, w_ref),
+        ])
+    ]
+    states_load = load(states_hbm, states_ref, 10)
+    for copy in gdn_loads:
+        copy.wait()
 
     def move(source, target, sent, received, seq, head):
         return pltpu.make_async_remote_copy(
@@ -136,7 +150,7 @@
         cols = slice(h * depth, (h + 1) * depth)
         if kind == 4:
             return stat_own.at[h], stat_buf.at[half, place]
-        source = (k_ref, v_ref, q_ref, dout_ref)[kind].at[:, cols]
+        source = (k_hbm, v_hbm, q_hbm, dout_hbm)[kind].at[:, cols]
         if kind < 2:
             return source, kv_buf.at[1 - half, kind, place_rows, :]
         return source, qd_buf.at[half, kind - 2, place_rows, :]
@@ -144,7 +158,7 @@
     def spread(h, kind):
         source, target = spread_refs(h, kind)
         return move(
-            source, target, a_send.at[h, kind], a_recv.at[place, kind],
+            source, target, sems.at[5 * h + kind], a_recv.at[place, kind],
             first + heads * core + h, pair + half,
         )
 
@@ -161,7 +175,7 @@
         else:
             target = qd_buf.at[own_qd, kind - 2, part_rows, :]
         return move(
-            target, target, a_send.at[0, kind], a_recv.at[block, kind], me, partner
+            target, target, sems.at[kind], a_recv.at[block, kind], me, partner
         )
 
     def start_spread(kinds):
@@ -193,7 +207,7 @@
     def hop(kind, m):
         return move(
             chunk(kind, slot(kind, m - 1, core)), chunk(kind, slot(kind, m, core)),
-            z_send.at[m - 1, kind], z_recv.at[m - 1, kind],
+            z_send.at[kind], z_recv.at[m - 1, kind],
             lax.rem(me + (size if kind < 2 else n - size), n), my_head,
         )
 
@@ -205,13 +219,17 @@
     def there(kind, m):
         return group >= m if kind < 2 else group + m < groups
 
+    def share_refs(kind, m, lane):
+        index = slot(kind, m, lane)
+        return kv_buf.at[index] if kind == 0 else qd_buf.at[index] if kind == 2 else stat_buf.at[index]
+
     def share(kind, m):
-        refs = chunk(kind, slot(kind, m, core))
-        return move(refs, refs, p_send.at[m, kind], p_recv.at[m, kind], me, partner)
+        refs = share_refs(kind, m, core)
+        return move(refs, refs, p_send.at[kind // 2], p_recv.at[m, kind // 2], me, partner)
 
     def share_in(kind, m):
-        refs = chunk(kind, slot(kind, m, 1 - core))
-        return move(refs, refs, p_send.at[m, kind], p_recv.at[m, kind], me, partner)
+        refs = share_refs(kind, m, 1 - core)
+        return move(refs, refs, p_send.at[kind // 2], p_recv.at[m, kind // 2], me, partner)
 
     def share_goes(kind, m):
         near, far = (0, 1) if kind < 2 else (1, 0)
@@ -239,42 +257,50 @@
         def _():
             getattr(copy, act)()
 
-    def send_on(kinds, m):
+    def pass_on(kind, m):
+        act_if(hop_goes(kind, m + 1), hop(kind, m + 1), "start")
+
+    def share_all(kinds, m):
         for kind in kinds:
+            if kind % 2 == 0:
+                if m:
+                    act_if(share_goes(kind, m - 1), share(kind, m - 1), "wait_send")
+                act_if(share_goes(kind, m), share(kind, m), "start")
+
+    def arrive(kinds, m, condition=True):
+        for kind in kinds:
+            act_if(there(kind, m) & condition(kind), hop(kind, m), "wait_recv")
             if m < steps:
-                act_if(hop_goes(kind, m + 1), hop(kind, m + 1), "start")
-        for kind in kinds:
-            act_if(share_goes(kind, m), share(kind, m), "start")
-
-    def arrive(kinds, m):
-        for kind in kinds:
-            act_if(there(kind, m), hop(kind, m), "wait_recv")
-            if m < steps:
-                act_if(hop_goes(kind, m + 1), hop(kind, m + 1), "start")
-            act_if(share_goes(kind, m), share(kind, m), "start")
+                act_if(hop_goes(kind, m) & condition(kind), hop(kind, m), "wait_send")
+                act_if(hop_goes(kind, m + 1) & condition(kind), hop(kind, m + 1), "start")
 
     w_rows = w_ref.shape[0]
 
     def w_copy(m):
         return move(
-            w_flat, w_all.at[me], w_send.at[m - 1], w_recv.at[0, m],
+            w_all.at[group, rank], w_all.at[group, rank], w_send.at[m - 1], w_recv.at[m - 1],
             lax.rem(me + m * size, n), my_head,
         )
 
-    def w_passes(i):
-        peer = first + lax.rem(rank + i, size)
-        return [
-            move(
-                w_flat if m == 0 else w_all.at[lax.rem(me + n - m * size, n)],
-                w_all.at[lax.rem(me + n - m * size, n)],
-                w_pass.at[i, m], w_recv.at[i, m], peer, my_head,
-            )
-            for m in range(groups)
-        ]
-
-    def each(copies, act):
-        for copy in copies:
-            getattr(copy, act)()
+    def w_in(m):
+        source = lax.rem(group + groups - m, groups)
+        return move(
+            w_all.at[source, rank], w_all.at[source, rank], w_send.at[m - 1], w_recv.at[m - 1],
+            me, partner,
+        )
+
+    def w_spread(j):
+        return move(
+            w_all.at[:, rank], w_all.at[:, rank], w_pass.at[j - 1], w_taken.at[j - 1],
+            first + lax.rem(rank + j, size), my_head,
+        )
+
+    def w_spread_in(j):
+        source = lax.rem(rank + size - j, size)
+        return move(
+            w_all.at[:, source], w_all.at[:, source], w_pass.at[j - 1], w_taken.at[j - 1],
+            me, partner,
+        )
 
     def ab_copy(h):
         return move(
@@ -288,49 +314,46 @@
             ab_buf.at[source], ab_buf.at[source], ab_send.at[0], ab_recv.at[source], me, partner
         )
 
+    def whole_copy():
+        return move(whole_out, whole_in, o_send, o_recv, lax.rem(me + n - size, n), my_head)
+
     def carry_copy():
-        return move(carry_out, carry_in, c_send, c_recv, lax.rem(me + n - size, n), my_head)
+        return move(
+            carry_out, carry_in, c_send, c_recv, lax.rem(me + 2 * n - 2 * size, n), my_head
+        )
 
     def adj_copy(j):
         target = lax.rem(rank + j, size)
         return move(
-            adj_out.at[target], adj_in.at[place], j_send.at[j - 1], j_recv.at[place],
+            adj_out.at[target], adj_in.at[place], sems.at[j - 1], j_recv.at[place],
             first + target, my_head,
         )
 
     def adj_arrival(h):
-        return move(adj_in.at[h], adj_in.at[h], j_send.at[0], j_recv.at[h], me, partner)
+        return move(adj_in.at[h], adj_in.at[h], sems.at[0], j_recv.at[h], me, partner)
 
     def back_rank(block):
         return core * heads + block
 
+    def part_of(item):
+        return slice(0, 1) if item == 0 else slice(1, 3)
+
     def back_copy(block, item):
         return move(
-            grad_out.at[item, block], grad_in.at[place, item],
-            t_send.at[block, item], t_recv.at[place, item],
+            grad_out.at[part_of(item), block], grad_in.at[place, part_of(item)],
+            sems.at[size + 2 * block + item], t_recv.at[place, item],
             first + back_rank(block), pair + half,
         )
 
     def back_here(block, item):
         return pltpu.make_async_copy(
-            grad_out.at[item, block], grad_in.at[place, item], t_recv.at[place, item]
+            grad_out.at[part_of(item), block], grad_in.at[place, part_of(item)],
+            t_recv.at[place, item],
         )
 
     def back_in(h, item):
-        return move(
-            grad_in.at[h, item], grad_in.at[h, item],
-            t_send.at[0, item], t_recv.at[h, item], me, partner,
-        )
-
-    def start_back(items):
-        for item in items:
-            for block in range(heads):
-                act_if(back_rank(block) == rank, back_here(block, item), "start")
-                act_if(back_rank(block) != rank, back_copy(block, item), "start")
-
-    start_spread(KEYS + QUERIES)
-    for m in range(1, groups):
-        w_copy(m).start()
+        refs = grad_in.at[h, part_of(item)]
+        return move(refs, refs, sems.at[size], t_recv.at[h, item], me, partner)
 
     row_ids = lax.broadcasted_iota(jnp.int32, (total, total), 0)
     col_ids = lax.broadcasted_iota(jnp.int32, (total, total), 1)
@@ -375,6 +398,24 @@
     lower = beta * faded_keys
     solved = jnp.where(eye, 1.0, 0.0) - lower
     powered = mm(lower, lower)
+
+    states_load.wait()
+    for copy in attention_loads:
+        copy.wait()
+    pl.semaphore_wait(barrier, greeted)
+    start_spread((0, 2, 1, 3))
+    ones = jnp.ones((8, depth), F32)
+    top = lax.broadcasted_iota(jnp.int32, (8, rows), 0) == 0
+    for h in range(heads):
+        cols = slice(h * depth, (h + 1) * depth)
+        product = dout_ref[:, cols].astype(F32) * out_ref[:, cols].astype(F32)
+        stat_own[h] = jnp.where(top, lse_ref[h : h + 1, :], mm_full(ones, product, NT))
+    start_spread((4,))
+    w_all[group, rank, :, :columns] = w_ref[:, 0, :]
+    w_all[group, rank, :, columns:] = w_ref[:, 1, :]
+    for m in range(1, groups):
+        w_copy(m).start()
+
     for step in range(BLOCK.bit_length() - 2):
         if step < BLOCK.bit_length() - 3:
             both = mm(jnp.concatenate([solved, powered], axis=0), powered)
@@ -422,10 +463,14 @@
 
         act_if(heads * core + h != rank, ab_copy(h), "start")
 
-    take_spread(KEYS)
-    send_on(KEYS, 0)
-    take_spread(QUERIES)
-    send_on(QUERIES, 0)
+    for kinds in ((0, 2), (1, 3, 4)):
+        take_spread(kinds)
+        for kind in kinds:
+            pass_on(kind, 0)
+    share_all(KEYS + QUERIES, 0)
+    for kind in KEYS + QUERIES:
+        for h in range(heads):
+            act_if(heads * core + h != rank, spread(h, kind), "wait_send")
 
     key_ids = row_ids
     query_ids = col_ids
@@ -482,16 +527,21 @@
             dk_acc[...] += dot(grad_logit, queries)
             dv_acc[...] += dot(weights, grads)
 
-    def attend_shared(d):
+    def take_shared_keys(d):
         for lane in range(2):
             m = (d + 1 - lane) // 2
-            for kind in KEYS:
-                act_if(share_comes(kind, m) & (core == lane), share_in(kind, m), "wait_recv")
-        attend_keys(d)
+            act_if(share_comes(0, m) & (core == lane), share_in(0, m), "wait_recv")
+
+    def take_shared_queries(d):
         for lane in range(2):
             m = (d + lane) // 2
-            for kind in QUERIES:
+            for kind in (2, 4):
                 act_if(share_comes(kind, m) & (core == lane), share_in(kind, m), "wait_recv")
+
+    def attend_shared(d):
+        take_shared_keys(d)
+        attend_keys(d)
+        take_shared_queries(d)
         attend_queries(d)
 
     pairs = [(h, b) for h in range(heads) for b in range(blocks)]
@@ -512,10 +562,9 @@
     unit_q_grad = growth * out_back + mm_once(faded_grad, unit_k)
     faded_back = mm_once(faded_grad, unit_q, TN)
 
-    for m in range(1, groups):
-        w_copy(m).wait_recv()
-    for i in range(1, size):
-        each(w_passes(i), "start")
+    relays = {kind: hop_goes(kind, 2) for kind in KEYS + QUERIES} if steps > 1 else {}
+    if steps > 1:
+        arrive((0, 2), 1, lambda kind: relays[kind])
 
     @pl.when(composer)
     def _():
@@ -534,56 +583,125 @@
             map_hi[r], map_lo[r] = split(joined[:, :depth])
             map_add[r] = joined[:, depth:]
 
+        @pl.when(group > 0)
+        def _():
+            whole_out[:, :depth] = (joined[:, :depth] - depth_eye).astype(BF16)
+            whole_out[:, depth:] = joined[:, depth:].astype(BF16)
+            whole_copy().start()
+
     def carry_step(condition):
         @pl.when(composer & condition)
         def _():
+            state_buf = adj_out.at[size - 1]
+
             @pl.when(group == groups - 1)
             def _():
-                carry_in[...] = jnp.zeros_like(carry_in)
-
-            act_if(group < groups - 1, carry_copy(), "wait_recv")
-            state = carry_in[...]
+                state_buf[...] = jnp.zeros_like(carry_in)
+
+            @pl.when(group < groups - 1)
+            def _():
+                whole_copy().wait_recv()
+
+            @pl.when(group == groups - 2)
+            def _():
+                state_buf[...] = whole_in[:, depth:]
+
+            @pl.when(group < groups - 2)
+            def _():
+                carry_copy().wait_recv()
+                carried = carry_in[...]
+                state_buf[...] = (
+                    carried.astype(F32)
+                    + (dot(whole_in[:, :depth], carried) + whole_in[:, depth:].astype(F32))
+                ).astype(BF16)
+
+            state = state_buf[...]
 
             def start_of(r):
                 return (dot(map_hi[r], state) + dot(map_lo[r], state) + map_add[r]).astype(BF16)
 
-            carry_out[...] = start_of(0)
-            act_if(group > 0, carry_copy(), "start")
+            @pl.when(group > 1)
+            def _():
+                carry_out[...] = start_of(0)
+                carry_copy().start()
+
             for r in range(size - 1):
                 adj_out[r] = start_of(r + 1)
-            adj_out[size - 1] = state
             for j in range(1, size):
                 adj_copy(j).start()
             adj_in[place] = adj_out[rank]
 
     last = groups - 1 - group
     carry_step(last == 0)
-    arrive(KEYS, 1)
-    arrive(QUERIES, 1)
+    for m in range(1, groups):
+        w_in(m).wait_recv()
+    for j in range(1, size):
+        w_spread(j).start()
+    if steps > 1:
+        arrive((0, 2), 1, lambda kind: jnp.logical_not(relays[kind]))
+    else:
+        arrive((0, 2), 1, lambda kind: True)
+    arrive((1, 3, 4), 1, lambda kind: True)
+    share_all(KEYS + QUERIES, 1)
     attend_keys(2)
     attend_queries(2)
     carry_step(last == 1)
     attend_shared(1)
+    carry_step(last == 2)
     for m in range(2, steps + 1):
-        arrive(KEYS, m)
-        arrive(QUERIES, m)
-    carry_step(last == 2)
+        arrive((0, 2, 1, 3, 4), m, lambda kind: True)
+        share_all(KEYS + QUERIES, m)
     for d in range(3, reach + 1):
         if d % 2:
-            attend_shared(d)
-        else:
-            attend_keys(d)
-            attend_queries(d)
+            take_shared_keys(d)
+        attend_keys(d)
 
     def blocks_of(matrix):
         return matrix.astype(BF16).reshape(heads, rows, depth)
 
+    def send_back(item):
+        for block in range(heads):
+            act_if(back_rank(block) == rank, back_here(block, item), "start")
+            act_if(back_rank(block) != rank, back_copy(block, item), "start")
+
+    grad_out[0] = blocks_of(dq_acc[...] * scaling)
+    send_back(0)
+    for d in range(3, reach + 1):
+        if d % 2:
+            take_shared_queries(d)
+        attend_queries(d)
     grad_out[1] = blocks_of(dk_acc[...] * scaling)
     grad_out[2] = blocks_of(dv_acc[...])
-    grad_out[0] = blocks_of(dq_acc[...] * scaling)
-    start_back((1, 2, 0))
+    send_back(1)
     carry_step(last >= 3)
 
+    for item in range(2):
+        for h in range(heads):
+            back_in(h, item).wait_recv()
+    for h in range(heads):
+        dq_out[:, h * depth : (h + 1) * depth] = grad_in[h, 0]
+    both_grads = jnp.concatenate(
+        [grad_in[h, item] for item in (1, 2) for h in range(heads)], axis=1
+    )
+    for j in range(1, size):
+        w_spread_in(j).wait_recv()
+    out_rows = dx_out.shape[0]
+    pieces_each = out_rows // (size * w_rows)
+
+    def dx_rows(owner):
+        piece = w_all[pl.ds(owner * pieces_each, pieces_each)].reshape(out_rows, 2 * columns)
+        return dot(piece, both_grads, NT)
+
+    def dx_copy(j):
+        return move(
+            dx_send.at[j - 1], dx_recv.at[j - 1], sems.at[size + 2 * heads + j - 1], x_recv.at[j - 1],
+            me, lax.rem(my_head + j, head_n),
+        )
+
+    for j in range(1, head_n):
+        dx_send[j - 1] = dx_rows(lax.rem(my_head + j, head_n))
+        dx_copy(j).start()
+    result = dx_rows(my_head)
     for h in range(heads):
         act_if(heads * core + h != rank, adj_arrival(h), "wait_recv")
     later = {}
@@ -638,66 +756,42 @@
         gdecay_out[h : h + 1, :] = decay_grad[:, own]
         gbeta_out[h : h + 1, :] = beta_row[:, own]
 
-    for item in (1, 2, 0):
-        for h in range(heads):
-            back_in(h, item).wait_recv()
-    for h in range(heads):
-        dq_out[:, h * depth : (h + 1) * depth] = grad_in[h, 0]
-    both_grads = jnp.concatenate(
-        [grad_in[h, item] for item in (1, 2) for h in range(heads)], axis=1
-    )
-    w_all[me] = w_flat[...]
-    for i in range(1, size):
-        each(w_passes(i), "wait_recv")
-    out_rows = dx_out.shape[0]
-    pieces_each = out_rows // w_rows
-
-    def dx_rows(owner):
-        piece = w_all[pl.ds(owner * pieces_each, pieces_each)].reshape(out_rows, 2 * columns)
-        return dot(piece, both_grads, NT)
-
-    def dx_copy(j):
-        return move(
-            dx_send.at[j - 1], dx_recv.at[j - 1], x_send.at[j - 1], x_recv.at[j - 1],
-            me, lax.rem(my_head + j, head_n),
-        )
-
-    for j in range(1, head_n):
-        dx_send[j - 1] = dx_rows(lax.rem(my_head + j, head_n))
-        dx_copy(j).start()
-    result = dx_rows(my_head)
     for j in range(1, head_n):
         dx_copy(j).wait_recv()
         result = result + dx_recv[j - 1]
     dx_out[...] = result.astype(BF16)
 
     for kind in KEYS + QUERIES:
-        for h in range(heads):
-            act_if(heads * core + h != rank, spread(h, kind), "wait_send")
-        for m in range(steps + 1):
-            if m:
-                act_if(hop_goes(kind, m), hop(kind, m), "wait_send")
-            act_if(share_goes(kind, m), share(kind, m), "wait_send")
+        act_if(hop_goes(kind, steps), hop(kind, steps), "wait_send")
+        if kind % 2 == 0:
+            act_if(share_goes(kind, steps), share(kind, steps), "wait_send")
     for m in range(1, groups):
         w_copy(m).wait_send()
-    for i in range(1, size):
-        each(w_passes(i), "wait_send")
+    for j in range(1, size):
+        w_spread(j).wait_send()
     for h in range(heads):
         act_if(heads * core + h != rank, ab_copy(h), "wait_send")
-    act_if(composer & (group > 0), carry_copy(), "wait_send")
+    act_if(composer & (group > 0), whole_copy(), "wait_send")
+    act_if(composer & (group > 1), carry_copy(), "wait_send")
     for j in range(1, size):
         act_if(composer, adj_copy(j), "wait_send")
-    for item in range(3):
-        for block in range(heads):
+    for block in range(heads):
+        for item in range(2):
             act_if(back_rank(block) != rank, back_copy(block, item), "wait_send")
     for j in range(1, head_n):
         dx_copy(j).wait_send()
 
 
 def hand_over(*refs):
-    half = len(refs) // 2
-    for source, target in zip(refs[:half], refs[half:]):
-        target[...] = source[...]
+    half = (len(refs) - 1) // 2
+    sems = refs[-1]
+    copies = [
+        pltpu.make_async_copy(refs[i], refs[half + i], sems.at[i]) for i in range(half)
+    ]
+    for copy in copies:
+        copy.start()
+    for copy in copies:
+        copy.wait()
 
 
 def per_device(n, head_n, *args):
@@ -720,28 +814,29 @@
     results = pl.pallas_call(
         functools.partial(kernel, n, head_n),
         out_shape=(
-            jax.ShapeDtypeStruct((rows, columns), BF16),
-            jax.ShapeDtypeStruct((out_rows, rows), BF16),
-            jax.ShapeDtypeStruct((rows, columns), BF16),
-            jax.ShapeDtypeStruct((rows, columns), BF16),
-            jax.ShapeDtypeStruct((rows, columns), BF16),
-            jax.ShapeDtypeStruct((heads, rows), F32),
-            jax.ShapeDtypeStruct((heads, rows), F32),
+            pltpu.VMEM((rows, columns), BF16),
+            pltpu.VMEM((out_rows, rows), BF16),
+            pltpu.VMEM((rows, columns), BF16),
+            pltpu.VMEM((rows, columns), BF16),
+            pltpu.VMEM((rows, columns), BF16),
+            pltpu.VMEM((heads, rows), F32),
+            pltpu.VMEM((heads, rows), F32),
         ),
-        in_specs=[vmem] * len(args),
+        in_specs=[pl.BlockSpec(memory_space=pl.ANY)] * len(args),
         out_specs=(vmem,) * 7,
-        scratch_shapes=[
+        scratch_shapes=[pltpu.VMEM(item.shape, item.dtype) for item in args[3:]] + [
             pltpu.VMEM((slots, 2, span, depth), BF16),
             pltpu.VMEM((slots, 2, span, depth), BF16),
             pltpu.VMEM((slots, heads, 8, rows), F32),
             pltpu.VMEM((heads, 8, rows), F32),
-            pltpu.VMEM((w_rows, 2 * columns), BF16),
-            pltpu.VMEM((n, w_rows, 2 * columns), BF16),
+            pltpu.VMEM((groups, size, w_rows, 2 * columns), BF16),
             pltpu.VMEM((heads, depth, 2 * depth), BF16),
             pltpu.VMEM((size, depth, 2 * depth), BF16),
             pltpu.VMEM((size, depth, depth), BF16),
             pltpu.VMEM((size, depth, depth), BF16),
             pltpu.VMEM((size, depth, depth), F32),
+            pltpu.VMEM((depth, 2 * depth), BF16),
+            pltpu.VMEM((depth, 2 * depth), BF16),
             pltpu.VMEM((depth, depth), BF16),
             pltpu.VMEM((depth, depth), BF16),
             pltpu.VMEM((size, depth, depth), BF16),
@@ -754,26 +849,28 @@
             pltpu.VMEM((span, depth), F32),
             pltpu.VMEM((span, depth), F32),
             pltpu.VMEM((heads, blocks, depth, 2 * depth), F32),
-            dma((heads, 5)), dma((heads, 5)),
-            dma((steps, 5)), dma((steps, 5)),
-            dma((steps + 1, 5)), dma((steps + 1, 5)),
-            dma((groups,)), dma((size, groups)), dma((size, groups)),
+            dma((max(5 * heads + 1, size + 2 * heads + others, 11),)), dma((heads, 5)),
+            dma((5,)), dma((steps, 5)),
+            dma((3,)), dma((steps + 1, 3)),
+            dma((groups,)), dma((groups,)), dma((size,)), dma((size,)),
             dma((heads,)), dma((size,)),
-            dma, dma,
-            dma((size,)), dma((heads,)),
-            dma((heads, 3)), dma((heads, 3)),
-            dma((others,)), dma((others,)),
+            dma, dma, dma, dma,
+            dma((heads,)),
+            dma((heads, 2)),
+            dma((others,)),
         ],
         compiler_params=pltpu.CompilerParams(
             collective_id=0, has_side_effects=True, vmem_limit_bytes=60000000
         ),
         name="layer_backward",
     )(*args)
+    results = [pltpu.with_memory_space_constraint(item, pltpu.VMEM) for item in results]
     return pl.pallas_call(
         hand_over,
         out_shape=[jax.ShapeDtypeStruct(item.shape, item.dtype) for item in results],
         in_specs=[vmem] * len(results),
-        out_specs=[vmem] * len(results),
+        out_specs=[pl.BlockSpec(memory_space=pl.ANY)] * len(results),
+        scratch_shapes=[dma((len(results),))],
         name="hand_over",
     )(*results)
 

time: 36.1 us -> 29.8 us (0.83)
  Pallas kernels: 35 us -> 29 us
    pallas_call x1, Pallas kernels: 33.3 us -> 28.2 us  [per_device(): pl.pallas_call(functools.partial(kernel, n, head_n), out_shape=(pltpu.VME...]
    pallas_call x1, Pallas kernels: 1.7 us -> 0.78 us  [per_device(): pl.pallas_call(hand_over, out_shape=[jax.ShapeDtypeStruct(item.shape, ite...]
where the time goes in v2:
time: 29.8 us; the launch traced here: 29.7 us
  Pallas kernels  29 us (97%)
  between operations  0.65 us (2%)
    pallas_call x1, Pallas kernels, per_device(): pl.pallas_call(functools.partial(kernel, n, head_n), out_shape=(pltpu.VME...  28.2 us
    pallas_call x1, Pallas kernels, per_device(): pl.pallas_call(hand_over, out_shape=[jax.ShapeDtypeStruct(item.shape, ite...  0.78 us

profile of v2, /device:TPU:0, one launch (start us, length us, event | category | flops | bytes accessed | tf_op | source)
XLA Modules:
  0.0 29.7 jit_solution(13448707641360871746)
XLA Ops:
  0.6 28.2 %layer_backward.1 = (bf16[128,256]{1,0:T(8,128)(2,1)S(1)}, bf16[256,128]{1,0:T(8,128)(2,1)S(1)}, bf16[128,256]{1,0:T(8,128)(2,1)S(1)}, bf16[128,256]{1,0:T(8,128...) custom-call(bf16[128,256]{1,0:T(8,128)(2,1)} %q_hbm.1, ...), custom_call_target="tpu_custom_call" | custom-call | tf_op jit(solution)/shard_map/layer_backward/pallas_call | solution.py:814
  28.9 0.8 %hand_over.1 = (bf16[128,256]{1,0:T(8,128)(2,1)}, bf16[256,128]{1,0:T(8,128)(2,1)}, bf16[128,256]{1,0:T(8,128)(2,1)}, bf16[128,256]{1,0:T(8,128)(2,1)}, bf16[128...) custom-call(bf16[128,256]{1,0:T(8,128)(2,1)S(1)} %get-tuple-element.14.refs_0_, ...), custom_call_target="tpu_custom_call" | custom-call | tf_op jit(solution)/shard_map/hand_over/pallas_call | solution.py:868

commit v3 on v2

--- a/solution.py
+++ b/solution.py
@@ -111,8 +111,11 @@
         greet({"seq": me, "head": lax.rem(my_head + j, head_n)})
     greeted = 2 * (size - 1) + groups - 1 + head_n - 1
 
+    spare = [ab_send.at[h] for h in range(heads)] + [p_send.at[i] for i in range(3)]
+    spare += [z_send.at[i] for i in range(5)] + [o_send]
+
     def load(source, target, index):
-        copy = pltpu.make_async_copy(source, target, sems.at[index])
+        copy = pltpu.make_async_copy(source, target, spare[index])
         copy.start()
         return copy
 
@@ -129,9 +132,7 @@
             (lse_hbm, lse_ref), (dout_hbm, dout_ref), (out_hbm, out_ref), (w_hbm, w_ref),
         ])
     ]
-    states_load = load(states_hbm, states_ref, 10)
-    for copy in gdn_loads:
-        copy.wait()
+    states_load = load(states_hbm, states_ref, len(spare) - 1)
 
     def move(source, target, sent, received, seq, head):
         return pltpu.make_async_remote_copy(
@@ -158,25 +159,17 @@
     def spread(h, kind):
         source, target = spread_refs(h, kind)
         return move(
-            source, target, sems.at[5 * h + kind], a_recv.at[place, kind],
+            source, target, sems.at[5 * h + kind], a_recv.at[kind],
             first + heads * core + h, pair + half,
         )
 
     def spread_here(h, kind):
         source, target = spread_refs(h, kind)
-        return pltpu.make_async_copy(source, target, a_recv.at[place, kind])
-
-    def spread_in(block, kind):
-        part_rows = slice(block * rows, (block + 1) * rows)
-        if kind == 4:
-            target = stat_buf.at[own_qd, block]
-        elif kind < 2:
-            target = kv_buf.at[own_kv, kind, part_rows, :]
-        else:
-            target = qd_buf.at[own_qd, kind - 2, part_rows, :]
-        return move(
-            target, target, sems.at[kind], a_recv.at[block, kind], me, partner
-        )
+        return pltpu.make_async_copy(source, target, a_recv.at[kind])
+
+    def spread_in(kind):
+        target = chunk(kind, slot(kind, 0, core))
+        return move(target, target, sems.at[kind], a_recv.at[kind], me, partner)
 
     def start_spread(kinds):
         for kind in kinds:
@@ -191,8 +184,7 @@
 
     def take_spread(kinds):
         for kind in kinds:
-            for block in range(heads):
-                spread_in(block, kind).wait_recv()
+            spread_in(kind).wait_recv()
 
     def chunk(kind, index):
         if kind == 4:
@@ -278,41 +270,33 @@
 
     def w_copy(m):
         return move(
-            w_all.at[group, rank], w_all.at[group, rank], w_send.at[m - 1], w_recv.at[m - 1],
+            w_all.at[group, rank], w_all.at[group, rank], w_send.at[m - 1], w_recv,
             lax.rem(me + m * size, n), my_head,
         )
 
-    def w_in(m):
-        source = lax.rem(group + groups - m, groups)
-        return move(
-            w_all.at[source, rank], w_all.at[source, rank], w_send.at[m - 1], w_recv.at[m - 1],
-            me, partner,
-        )
+    def w_in():
+        refs = w_all.at[0 : groups - 1, rank]
+        return move(refs, refs, w_send.at[0], w_recv, me, partner)
 
     def w_spread(j):
         return move(
-            w_all.at[:, rank], w_all.at[:, rank], w_pass.at[j - 1], w_taken.at[j - 1],
+            w_all.at[:, rank], w_all.at[:, rank], w_pass.at[j - 1], w_taken,
             first + lax.rem(rank + j, size), my_head,
         )
 
-    def w_spread_in(j):
-        source = lax.rem(rank + size - j, size)
-        return move(
-            w_all.at[:, source], w_all.at[:, source], w_pass.at[j - 1], w_taken.at[j - 1],
-            me, partner,
-        )
+    def w_spread_in():
+        refs = w_all.at[:, 0 : size - 1]
+        return move(refs, refs, w_pass.at[0], w_taken, me, partner)
 
     def ab_copy(h):
         return move(
-            ab_send_buf.at[h], ab_buf.at[rank], ab_send.at[h], ab_recv.at[rank],
+            ab_send_buf.at[h], ab_buf.at[rank], ab_send.at[h], ab_recv,
             first + heads * core + h, my_head,
         )
 
-    def ab_in(j):
-        source = lax.rem(rank + j, size)
-        return move(
-            ab_buf.at[source], ab_buf.at[source], ab_send.at[0], ab_recv.at[source], me, partner
-        )
+    def ab_in():
+        refs = ab_buf.at[0 : size - 1]
+        return move(refs, refs, ab_send.at[0], ab_recv, me, partner)
 
     def whole_copy():
         return move(whole_out, whole_in, o_send, o_recv, lax.rem(me + n - size, n), my_head)
@@ -341,22 +325,30 @@
     def back_copy(block, item):
         return move(
             grad_out.at[part_of(item), block], grad_in.at[place, part_of(item)],
-            sems.at[size + 2 * block + item], t_recv.at[place, item],
+            sems.at[size + 2 * block + item], t_recv.at[item],
             first + back_rank(block), pair + half,
         )
 
     def back_here(block, item):
         return pltpu.make_async_copy(
             grad_out.at[part_of(item), block], grad_in.at[place, part_of(item)],
-            t_recv.at[place, item],
-        )
-
-    def back_in(h, item):
-        refs = grad_in.at[h, part_of(item)]
-        return move(refs, refs, sems.at[size], t_recv.at[h, item], me, partner)
-
-    row_ids = lax.broadcasted_iota(jnp.int32, (total, total), 0)
-    col_ids = lax.broadcasted_iota(jnp.int32, (total, total), 1)
+            t_recv.at[item],
+        )
+
+    def back_in(item):
+        refs = grad_in.at[:, part_of(item)]
+        return move(refs, refs, sems.at[size], t_recv.at[item], me, partner)
+
+    def open_links():
+        pl.semaphore_wait(barrier, greeted)
+        start_spread((0, 2, 1, 3))
+
+    pl.when(half == 1)(open_links)
+    for copy in gdn_loads:
+        copy.wait()
+
+    row_ids = lax.broadcasted_iota(jnp.int32, (rows, rows), 0)
+    col_ids = lax.broadcasted_iota(jnp.int32, (rows, rows), 1)
     shift = BLOCK.bit_length() - 1
     same = lax.shift_right_logical(row_ids, shift) == lax.shift_right_logical(col_ids, shift)
     eye = row_ids == col_ids
@@ -369,41 +361,53 @@
     def to_row(column):
         return column_sum(jnp.where(eye, column, 0.0))
 
-    def flat_row(ref):
-        return jnp.concatenate([ref[h : h + 1, :] for h in range(heads)], axis=1)
-
-    decay_row = flat_row(decay_ref)
-    decay_col = to_column(decay_row)
-    beta = to_column(flat_row(beta_ref))
-    summed = row_sum(jnp.where(causal, decay_row, 0.0))
-    summed_row = column_sum(jnp.where(same & (row_ids <= col_ids), decay_col, 0.0))
-    whole = row_sum(jnp.where(same, decay_row, 0.0))
-    growth = jnp.exp(summed)
-    tail = jnp.exp(row_sum(jnp.where(same & (row_ids < col_ids), decay_row, 0.0)))
-    end_growth = jnp.exp(whole)
-    raw_q = stack_heads(gq_ref[...], heads).astype(F32)
-    raw_k = stack_heads(gk_ref[...], heads).astype(F32)
-    values = stack_heads(gv_ref[...], heads).astype(F32)
-    out_grad = stack_heads(gdo_ref[...], heads).astype(F32)
-    inv_q = lax.rsqrt(row_sum(raw_q * raw_q) + EPS)
-    inv_k = lax.rsqrt(row_sum(raw_k * raw_k) + EPS)
-    unit_q = raw_q * inv_q * scaling
-    unit_k = raw_k * inv_k
-    fading = jnp.where(causal, jnp.exp(jnp.where(causal, summed - summed_row, 0.0)), 0.0)
-    products = mm(jnp.concatenate([unit_k, unit_q], axis=0), unit_k, NT)
-    key_products = products[:total]
-    query_products = products[total:]
-    strict_fading = jnp.where(strict, fading, 0.0)
-    faded_keys = strict_fading * key_products
-    lower = beta * faded_keys
-    solved = jnp.where(eye, 1.0, 0.0) - lower
-    powered = mm(lower, lower)
-
-    states_load.wait()
+    def per_head(function, *lists):
+        return [function(*items) for items in zip(*lists)]
+
+    def cut(ref):
+        return [ref[:, h * depth : (h + 1) * depth].astype(F32) for h in range(heads)]
+
+    decay_row = [decay_ref[h : h + 1, :] for h in range(heads)]
+    decay_col = per_head(to_column, decay_row)
+    beta = [to_column(beta_ref[h : h + 1, :]) for h in range(heads)]
+    summed = [row_sum(jnp.where(causal, row, 0.0)) for row in decay_row]
+    summed_row = [column_sum(jnp.where(same & (row_ids <= col_ids), col, 0.0)) for col in decay_col]
+    raw_q = cut(gq_ref)
+    raw_k = cut(gk_ref)
+    inv_q = [lax.rsqrt(row_sum(raw * raw) + EPS) for raw in raw_q]
+    inv_k = [lax.rsqrt(row_sum(raw * raw) + EPS) for raw in raw_k]
+    unit_q = [raw * inv * scaling for raw, inv in zip(raw_q, inv_q)]
+    unit_k = [raw * inv for raw, inv in zip(raw_k, inv_k)]
+    fading = per_head(
+        lambda col, row: jnp.where(causal, jnp.exp(jnp.where(causal, col - row, 0.0)), 0.0),
+        summed, summed_row,
+    )
+    products = [
+        mm(jnp.concatenate([k, q], axis=0), k, NT) for k, q in zip(unit_k, unit_q)
+    ]
+    key_products = [item[:rows] for item in products]
+    query_products = [item[rows:] for item in products]
+    strict_fading = [jnp.where(strict, item, 0.0) for item in fading]
+    faded_keys = per_head(lambda a, b: a * b, strict_fading, key_products)
+    lower = per_head(lambda a, b: a * b, beta, faded_keys)
+
+    def pack(matrix):
+        packed = matrix[:BLOCK]
+        for b in range(1, blocks):
+            packed = packed + matrix[b * BLOCK : (b + 1) * BLOCK]
+        return packed
+
+    def unpack(packed):
+        return jnp.where(same, jnp.concatenate([packed] * blocks, axis=0), 0.0)
+
+    packed = per_head(pack, lower)
+    unit = pack(jnp.where(eye, 1.0, 0.0))
+    solved = [unit - item for item in packed]
+    powered = per_head(mm, packed, lower)
+
+    pl.when(half == 0)(open_links)
     for copy in attention_loads:
         copy.wait()
-    pl.semaphore_wait(barrier, greeted)
-    start_spread((0, 2, 1, 3))
     ones = jnp.ones((8, depth), F32)
     top = lax.broadcasted_iota(jnp.int32, (8, rows), 0) == 0
     for h in range(heads):
@@ -417,21 +421,32 @@
         w_copy(m).start()
 
     for step in range(BLOCK.bit_length() - 2):
+        wide = per_head(unpack, powered)
         if step < BLOCK.bit_length() - 3:
-            both = mm(jnp.concatenate([solved, powered], axis=0), powered)
-            solved = solved + both[:total]
-            powered = both[total:]
+            both = [
+                mm(jnp.concatenate([a, b], axis=0), c) for a, b, c in zip(solved, powered, wide)
+            ]
+            solved = [a + b[:BLOCK] for a, b in zip(solved, both)]
+            powered = [b[BLOCK:] for b in both]
         else:
-            solved = solved + mm(solved, powered)
-    attention = fading * query_products
-    widened = mm(solved, (beta * growth) * unit_k)
-    pulled = mm(attention, out_grad, TN)
-    tailing = tail * unit_k
-    grown_q = growth * unit_q
+            solved = [a + mm(a, c) for a, c in zip(solved, wide)]
+    solved = per_head(unpack, solved)
+
+    whole = [row_sum(jnp.where(same, row, 0.0)) for row in decay_row]
+    growth = per_head(jnp.exp, summed)
+    tail = [
+        jnp.exp(row_sum(jnp.where(same & (row_ids < col_ids), row, 0.0))) for row in decay_row
+    ]
+    end_growth = per_head(jnp.exp, whole)
+    out_grad = cut(gdo_ref)
+    attention = per_head(lambda a, b: a * b, fading, query_products)
+    widened = [mm(s, (b * g) * k) for s, b, g, k in zip(solved, beta, growth, unit_k)]
+    pulled = per_head(lambda a, o: mm(a, o, TN), attention, out_grad)
+    tailing = per_head(lambda a, b: a * b, tail, unit_k)
+    grown_q = per_head(lambda a, b: a * b, growth, unit_q)
 
     def part(matrix, h, b):
-        start = h * rows + b * BLOCK
-        return matrix[start : start + BLOCK]
+        return matrix[h][b * BLOCK : (b + 1) * BLOCK]
 
     depth_eye = jnp.where(
         lax.broadcasted_iota(jnp.int32, (depth, depth), 0)
@@ -439,6 +454,7 @@
         1.0,
         0.0,
     )
+    ends = []
     for h in range(heads):
         across = None
         for b in reversed(range(blocks)):
@@ -454,6 +470,9 @@
             else:
                 joined = mm(carry_map, jnp.concatenate([across, offset], axis=1))
                 across, offset = joined[:, :depth], joined[:, depth:] + local
+        ends.append((across, offset))
+    for h in range(heads):
+        across, offset = ends[h]
         change = jnp.concatenate([across - depth_eye, offset], axis=1).astype(BF16)
         ab_send_buf[h] = change
 
@@ -462,6 +481,31 @@
             ab_buf[rank] = change
 
         act_if(heads * core + h != rank, ab_copy(h), "start")
+
+    def by_parts(make):
+        return [
+            jnp.concatenate([make(h, b) for b in range(blocks)], axis=0) for h in range(heads)
+        ]
+
+    values = cut(gv_ref)
+    states_load.wait()
+    reads = [
+        [
+            mm(jnp.concatenate([part(unit_k, h, b), part(unit_q, h, b)], axis=0), states_ref[b, h])
+            for b in range(blocks)
+        ]
+        for h in range(heads)
+    ]
+    key_reads = [jnp.concatenate([item[:BLOCK] for item in row], axis=0) for row in reads]
+    query_reads = [jnp.concatenate([item[BLOCK:] for item in row], axis=0) for row in reads]
+    remainder = [v - g * r for v, g, r in zip(values, growth, key_reads)]
+    fresh = [mm(s, b * r) for s, b, r in zip(solved, beta, remainder)]
+    faded_grad = [f * mm(o, r, NT) for f, o, r in zip(fading, out_grad, fresh)]
+    out_back = by_parts(lambda h, b: mm_once(part(out_grad, h, b), states_ref[b, h], NT))
+    unit_q_grad = [
+        g * o + mm_once(f, k) for g, o, f, k in zip(growth, out_back, faded_grad, unit_k)
+    ]
+    faded_back = [mm_once(f, q, TN) for f, q in zip(faded_grad, unit_q)]
 
     for kinds in ((0, 2), (1, 3, 4)):
         take_spread(kinds)
@@ -472,8 +516,8 @@
         for h in range(heads):
             act_if(heads * core + h != rank, spread(h, kind), "wait_send")
 
-    key_ids = row_ids
-    query_ids = col_ids
+    key_ids = lax.broadcasted_iota(jnp.int32, (total, total), 0)
+    query_ids = lax.broadcasted_iota(jnp.int32, (total, total), 1)
 
     def stat_row(index, which):
         return jnp.concatenate(
@@ -500,8 +544,18 @@
     dq_acc[...] = dot(grad_logit, keys, TN)
     dk_acc[...] = dot(grad_logit, queries)
     dv_acc[...] = dot(weights, grads)
-    lse_column = to_column(own_lse)
-    dots_column = to_column(own_dots)
+
+    def stat_column(which):
+        return jnp.concatenate(
+            [
+                to_column(stat_buf[own_qd, block, which : which + 1, :])
+                for block in range(heads)
+            ],
+            axis=0,
+        )
+
+    lse_column = stat_column(0)
+    dots_column = stat_column(1)
 
     def attend_keys(d):
         @pl.when(2 * group + core >= d)
@@ -510,7 +564,7 @@
             grad_logit, _ = terms(
                 dot(qd_buf[own_qd, 0], keys, NT),
                 dot(qd_buf[own_qd, 1], kv_buf[d + 1 - core, 1], NT),
-                lse_column, dots_column, row_ids < col_ids if d == reach else None,
+                lse_column, dots_column, key_ids < query_ids if d == reach else None,
             )
             dq_acc[...] += dot(grad_logit, keys)
 
@@ -544,24 +598,6 @@
         take_shared_queries(d)
         attend_queries(d)
 
-    pairs = [(h, b) for h in range(heads) for b in range(blocks)]
-
-    def by_parts(make):
-        return jnp.concatenate([make(h, b) for h, b in pairs], axis=0)
-
-    reads = [
-        mm(jnp.concatenate([part(unit_k, h, b), part(unit_q, h, b)], axis=0), states_ref[b, h])
-        for h, b in pairs
-    ]
-    key_reads = jnp.concatenate([item[:BLOCK] for item in reads], axis=0)
-    query_reads = jnp.concatenate([item[BLOCK:] for item in reads], axis=0)
-    remainder = values - growth * key_reads
-    fresh = mm(solved, beta * remainder)
-    faded_grad = fading * mm(out_grad, fresh, NT)
-    out_back = by_parts(lambda h, b: mm_once(part(out_grad, h, b), states_ref[b, h], NT))
-    unit_q_grad = growth * out_back + mm_once(faded_grad, unit_k)
-    faded_back = mm_once(faded_grad, unit_q, TN)
-
     relays = {kind: hop_goes(kind, 2) for kind in KEYS + QUERIES} if steps > 1 else {}
     if steps > 1:
         arrive((0, 2), 1, lambda kind: relays[kind])
@@ -569,8 +605,7 @@
     @pl.when(composer)
     def _():
         joined = None
-        for j in range(1, size):
-            ab_in(j).wait_recv()
+        ab_in().wait_recv()
         for r in reversed(range(size)):
             change = ab_buf[r, :, :depth]
             local = ab_buf[r, :, depth:].astype(F32)
@@ -633,8 +668,8 @@
 
     last = groups - 1 - group
     carry_step(last == 0)
-    for m in range(1, groups):
-        w_in(m).wait_recv()
+    if groups > 1:
+        w_in().wait_recv()
     for j in range(1, size):
         w_spread(j).start()
     if steps > 1:
@@ -648,6 +683,20 @@
     carry_step(last == 1)
     attend_shared(1)
     carry_step(last == 2)
+
+    def blocks_of(matrix):
+        return matrix.astype(BF16).reshape(heads, rows, depth)
+
+    def send_back(item):
+        for block in range(heads):
+            act_if(back_rank(block) == rank, back_here(block, item), "start")
+            act_if(back_rank(block) != rank, back_copy(block, item), "start")
+
+    def send_queries():
+        grad_out[0] = blocks_of(dq_acc[...] * scaling)
+        send_back(0)
+
+    pl.when(group == 0)(send_queries)
     for m in range(2, steps + 1):
         arrive((0, 2, 1, 3, 4), m, lambda kind: True)
         share_all(KEYS + QUERIES, m)
@@ -656,16 +705,7 @@
             take_shared_keys(d)
         attend_keys(d)
 
-    def blocks_of(matrix):
-        return matrix.astype(BF16).reshape(heads, rows, depth)
-
-    def send_back(item):
-        for block in range(heads):
-            act_if(back_rank(block) == rank, back_here(block, item), "start")
-            act_if(back_rank(block) != rank, back_copy(block, item), "start")
-
-    grad_out[0] = blocks_of(dq_acc[...] * scaling)
-    send_back(0)
+    pl.when(group > 0)(send_queries)
     for d in range(3, reach + 1):
         if d % 2:
             take_shared_queries(d)
@@ -676,15 +716,13 @@
     carry_step(last >= 3)
 
     for item in range(2):
-        for h in range(heads):
-            back_in(h, item).wait_recv()
+        back_in(item).wait_recv()
     for h in range(heads):
         dq_out[:, h * depth : (h + 1) * depth] = grad_in[h, 0]
     both_grads = jnp.concatenate(
         [grad_in[h, item] for item in (1, 2) for h in range(heads)], axis=1
     )
-    for j in range(1, size):
-        w_spread_in(j).wait_recv()
+    w_spread_in().wait_recv()
     out_rows = dx_out.shape[0]
     pieces_each = out_rows // (size * w_rows)
 
@@ -711,50 +749,49 @@
             later[h, b] = adjoint
             if b > 0:
                 adjoint = mm(map_buf[h, b, :, :depth], adjoint) + map_buf[h, b, :, depth:]
-    fresh_grad = pulled + by_parts(lambda h, b: mm(part(tailing, h, b), later[h, b]))
-    solved_grad = mm(solved, fresh_grad, TN)
-    lower_grad = -mm(solved_grad, fresh, NT)
-    key_products_grad = beta * strict_fading * lower_grad
-    value_grad = beta * solved_grad
+    moved = by_parts(lambda h, b: mm(part(tailing, h, b), later[h, b]))
+    fresh_grad = per_head(lambda a, b: a + b, pulled, moved)
+    solved_grad = [mm(s, f, TN) for s, f in zip(solved, fresh_grad)]
+    lower_grad = [-mm(s, f, NT) for s, f in zip(solved_grad, fresh)]
+    key_products_grad = [b * f * g for b, f, g in zip(beta, strict_fading, lower_grad)]
+    value_grad = per_head(lambda a, b: a * b, beta, solved_grad)
     value_back = by_parts(lambda h, b: mm_once(part(value_grad, h, b), states_ref[b, h], NT))
-    fresh_back = tail * by_parts(lambda h, b: mm(part(fresh, h, b), later[h, b], NT))
-    unit_k_grad = (
-        fresh_back
-        - growth * value_back
-        + faded_back
-        + mm_once(key_products_grad, unit_k)
-        + mm_once(key_products_grad, unit_k, TN)
-    )
-    q_grad = scaling * inv_q * (unit_q_grad - raw_q * (inv_q * inv_q * row_sum(unit_q_grad * raw_q)))
-    k_grad = inv_k * (unit_k_grad - raw_k * (inv_k * inv_k * row_sum(unit_k_grad * raw_k)))
+    fresh_moved = by_parts(lambda h, b: mm(part(fresh, h, b), later[h, b], NT))
+    fresh_back = per_head(lambda a, b: a * b, tail, fresh_moved)
     for h in range(heads):
         cols = slice(h * depth, (h + 1) * depth)
-        own = slice(h * rows, (h + 1) * rows)
-        gdq_out[:, cols] = q_grad[own].astype(BF16)
-        gdk_out[:, cols] = k_grad[own].astype(BF16)
-        gdv_out[:, cols] = value_grad[own].astype(BF16)
-    beta_grad = row_sum(solved_grad * remainder) + row_sum(lower_grad * faded_keys)
-    exponent = faded_grad * query_products + key_products_grad * key_products
-    tail_grad = row_sum(unit_k * fresh_back)
-    growth_grad = row_sum(out_grad * query_reads) - row_sum(value_grad * key_reads)
-    summed_grad = (
-        row_sum(exponent) - to_column(column_sum(exponent)) - tail_grad + growth * growth_grad
-    )
-    end_grad = end_growth * by_parts(
-        lambda h, b: jnp.broadcast_to(
-            column_sum(row_sum(later[h, b] * states_ref[b, h])), (BLOCK, 1)
-        )
-    )
-    decay_grad = (
-        column_sum(jnp.where(causal, summed_grad, 0.0))
-        + column_sum(jnp.where(same, tail_grad, 0.0))
-        + to_row(end_grad)
-    )
-    beta_row = to_row(beta_grad)
-    for h in range(heads):
-        own = slice(h * rows, (h + 1) * rows)
-        gdecay_out[h : h + 1, :] = decay_grad[:, own]
-        gbeta_out[h : h + 1, :] = beta_row[:, own]
+        unit_k_grad = (
+            fresh_back[h]
+            - growth[h] * value_back[h]
+            + faded_back[h]
+            + mm_once(key_products_grad[h], unit_k[h])
+            + mm_once(key_products_grad[h], unit_k[h], TN)
+        )
+        q_share = inv_q[h] * inv_q[h] * row_sum(unit_q_grad[h] * raw_q[h])
+        k_share = inv_k[h] * inv_k[h] * row_sum(unit_k_grad * raw_k[h])
+        gdq_out[:, cols] = (scaling * inv_q[h] * (unit_q_grad[h] - raw_q[h] * q_share)).astype(BF16)
+        gdk_out[:, cols] = (inv_k[h] * (unit_k_grad - raw_k[h] * k_share)).astype(BF16)
+        gdv_out[:, cols] = value_grad[h].astype(BF16)
+        beta_grad = row_sum(solved_grad[h] * remainder[h]) + row_sum(lower_grad[h] * faded_keys[h])
+        exponent = faded_grad[h] * query_products[h] + key_products_grad[h] * key_products[h]
+        tail_grad = row_sum(unit_k[h] * fresh_back[h])
+        growth_grad = row_sum(out_grad[h] * query_reads[h]) - row_sum(value_grad[h] * key_reads[h])
+        summed_grad = (
+            row_sum(exponent) - to_column(column_sum(exponent)) - tail_grad + growth[h] * growth_grad
+        )
+        end_grad = end_growth[h] * jnp.concatenate(
+            [
+                jnp.broadcast_to(column_sum(row_sum(later[h, b] * states_ref[b, h])), (BLOCK, 1))
+                for b in range(blocks)
+            ],
+            axis=0,
+        )
+        gdecay_out[h : h + 1, :] = (
+            column_sum(jnp.where(causal, summed_grad, 0.0))
+            + column_sum(jnp.where(same, tail_grad, 0.0))
+            + to_row(end_grad)
+        )
+        gbeta_out[h : h + 1, :] = to_row(beta_grad)
 
     for j in range(1, head_n):
         dx_copy(j).wait_recv()
@@ -849,14 +886,14 @@
             pltpu.VMEM((span, depth), F32),
             pltpu.VMEM((span, depth), F32),
             pltpu.VMEM((heads, blocks, depth, 2 * depth), F32),
-            dma((max(5 * heads + 1, size + 2 * heads + others, 11),)), dma((heads, 5)),
+            dma((max(5 * heads, size + 2 * heads + others),)), dma((5,)),
             dma((5,)), dma((steps, 5)),
             dma((3,)), dma((steps + 1, 3)),
-            dma((groups,)), dma((groups,)), dma((size,)), dma((size,)),
-            dma((heads,)), dma((size,)),
+            dma((max(groups - 1, 1),)), dma, dma((size - 1,)), dma,
+            dma((heads,)), dma,
             dma, dma, dma, dma,
             dma((heads,)),
-            dma((heads, 2)),
+            dma((2,)),
             dma((others,)),
         ],
         compiler_params=pltpu.CompilerParams(

time: 29.8 us -> 27.8 us (0.933)
  Pallas kernels: 29 us -> 27 us
    pallas_call x1, Pallas kernels: 28.2 us -> 26.3 us  [per_device(): pl.pallas_call(functools.partial(kernel, n, head_n), out_shape=(pltpu.VME...]
where the time goes in v3:
time: 27.8 us; the launch traced here: 27.7 us
  Pallas kernels  27 us (97%)
  between operations  0.65 us (2%)
    pallas_call x1, Pallas kernels, per_device(): pl.pallas_call(functools.partial(kernel, n, head_n), out_shape=(pltpu.VME...  26.3 us
    pallas_call x1, Pallas kernels, per_device(): pl.pallas_call(hand_over, out_shape=[jax.ShapeDtypeStruct(item.shape, ite...  0.78 us

profile of v3, /device:TPU:0, one launch (start us, length us, event | category | flops | bytes accessed | tf_op | source)
XLA Modules:
  0.0 27.7 jit_solution(8001162178709804796)
XLA Ops:
  0.6 26.3 %layer_backward.1 = (bf16[128,256]{1,0:T(8,128)(2,1)S(1)}, bf16[256,128]{1,0:T(8,128)(2,1)S(1)}, bf16[128,256]{1,0:T(8,128)(2,1)S(1)}, bf16[128,256]{1,0:T(8,128...) custom-call(bf16[128,256]{1,0:T(8,128)(2,1)} %q_hbm.1, ...), custom_call_target="tpu_custom_call" | custom-call | tf_op jit(solution)/shard_map/layer_backward/pallas_call | solution.py:851
  26.9 0.8 %hand_over.1 = (bf16[128,256]{1,0:T(8,128)(2,1)}, bf16[256,128]{1,0:T(8,128)(2,1)}, bf16[128,256]{1,0:T(8,128)(2,1)}, bf16[128,256]{1,0:T(8,128)(2,1)}, bf16[128...) custom-call(bf16[128,256]{1,0:T(8,128)(2,1)S(1)} %get-tuple-element.14.refs_0_, ...), custom_call_target="tpu_custom_call" | custom-call | tf_op jit(solution)/shard_map/hand_over/pallas_call | solution.py:905

commit v4 on v3

--- a/solution.py
+++ b/solution.py
@@ -306,10 +306,9 @@
             carry_out, carry_in, c_send, c_recv, lax.rem(me + 2 * n - 2 * size, n), my_head
         )
 
-    def adj_copy(j):
-        target = lax.rem(rank + j, size)
+    def adj_copy(target):
         return move(
-            adj_out.at[target], adj_in.at[place], sems.at[j - 1], j_recv.at[place],
+            adj_out.at[target], adj_in.at[place], sems.at[target], j_recv.at[place],
             first + target, my_head,
         )
 
@@ -624,6 +623,11 @@
             whole_out[:, depth:] = joined[:, depth:].astype(BF16)
             whole_copy().start()
 
+    if groups > 1:
+        w_in().wait_recv()
+    for j in range(1, size):
+        w_spread(j).start()
+
     def carry_step(condition):
         @pl.when(composer & condition)
         def _():
@@ -662,16 +666,12 @@
 
             for r in range(size - 1):
                 adj_out[r] = start_of(r + 1)
-            for j in range(1, size):
-                adj_copy(j).start()
+            for r in range(size):
+                act_if(rank != r, adj_copy(r), "start")
             adj_in[place] = adj_out[rank]
 
     last = groups - 1 - group
     carry_step(last == 0)
-    if groups > 1:
-        w_in().wait_recv()
-    for j in range(1, size):
-        w_spread(j).start()
     if steps > 1:
         arrive((0, 2), 1, lambda kind: jnp.logical_not(relays[kind]))
     else:
@@ -810,8 +810,8 @@
         act_if(heads * core + h != rank, ab_copy(h), "wait_send")
     act_if(composer & (group > 0), whole_copy(), "wait_send")
     act_if(composer & (group > 1), carry_copy(), "wait_send")
-    for j in range(1, size):
-        act_if(composer, adj_copy(j), "wait_send")
+    for r in range(size):
+        act_if(composer & (rank != r), adj_copy(r), "wait_send")
     for block in range(heads):
         for item in range(2):
             act_if(back_rank(block) != rank, back_copy(block, item), "wait_send")

time: 27.8 us -> 27.5 us (0.989)
  Pallas kernels: 27 us -> 26.7 us
    pallas_call x1, Pallas kernels: 26.3 us -> 25.9 us  [per_device(): pl.pallas_call(functools.partial(kernel, n, head_n), out_shape=(pltpu.VME...]
where the time goes in v4:
time: 27.5 us; the launch traced here: 27.3 us
  Pallas kernels  26.7 us (97%)
  between operations  0.65 us (2%)
    pallas_call x1, Pallas kernels, per_device(): pl.pallas_call(functools.partial(kernel, n, head_n), out_shape=(pltpu.VME...  25.9 us
    pallas_call x1, Pallas kernels, per_device(): pl.pallas_call(hand_over, out_shape=[jax.ShapeDtypeStruct(item.shape, ite...  0.78 us

profile of v4, /device:TPU:0, one launch (start us, length us, event | category | flops | bytes accessed | tf_op | source)
XLA Modules:
  0.0 27.3 jit_solution(832773979722802976)
XLA Ops:
  0.6 25.9 %layer_backward.1 = (bf16[128,256]{1,0:T(8,128)(2,1)S(1)}, bf16[256,128]{1,0:T(8,128)(2,1)S(1)}, bf16[128,256]{1,0:T(8,128)(2,1)S(1)}, bf16[128,256]{1,0:T(8,128...) custom-call(bf16[128,256]{1,0:T(8,128)(2,1)} %q_hbm.1, ...), custom_call_target="tpu_custom_call" | custom-call | tf_op jit(solution)/shard_map/layer_backward/pallas_call | solution.py:851
  26.5 0.8 %hand_over.1 = (bf16[128,256]{1,0:T(8,128)(2,1)}, bf16[256,128]{1,0:T(8,128)(2,1)}, bf16[128,256]{1,0:T(8,128)(2,1)}, bf16[128,256]{1,0:T(8,128)(2,1)}, bf16[128...) custom-call(bf16[128,256]{1,0:T(8,128)(2,1)S(1)} %get-tuple-element.14.refs_0_, ...), custom_call_target="tpu_custom_call" | custom-call | tf_op jit(solution)/shard_map/hand_over/pallas_call | solution.py:905

commit v5 on v4

--- a/solution.py
+++ b/solution.py
@@ -112,7 +112,7 @@
     greeted = 2 * (size - 1) + groups - 1 + head_n - 1
 
     spare = [ab_send.at[h] for h in range(heads)] + [p_send.at[i] for i in range(3)]
-    spare += [z_send.at[i] for i in range(5)] + [o_send]
+    spare += [z_send.at[i] for i in range(5)] + [o_send.at[0]]
 
     def load(source, target, index):
         copy = pltpu.make_async_copy(source, target, spare[index])
@@ -298,8 +298,11 @@
         refs = ab_buf.at[0 : size - 1]
         return move(refs, refs, ab_send.at[0], ab_recv, me, partner)
 
-    def whole_copy():
-        return move(whole_out, whole_in, o_send, o_recv, lax.rem(me + n - size, n), my_head)
+    def whole_copy(side):
+        return move(
+            whole_out.at[side], whole_in.at[side], o_send.at[side], o_recv.at[side],
+            lax.rem(me + n - size, n), my_head,
+        )
 
     def carry_copy():
         return move(
@@ -556,8 +559,10 @@
     lse_column = stat_column(0)
     dots_column = stat_column(1)
 
-    def attend_keys(d):
-        @pl.when(2 * group + core >= d)
+    def attend_keys(d, lanes=(0, 1)):
+        lane_here = (2 * group + core >= d) & ((core == lanes[0]) | (core == lanes[-1]))
+
+        @pl.when(lane_here)
         def _():
             keys = kv_buf[d + 1 - core, 0]
             grad_logit, _ = terms(
@@ -567,8 +572,12 @@
             )
             dq_acc[...] += dot(grad_logit, keys)
 
-    def attend_queries(d):
-        @pl.when(2 * group + core + d < 2 * groups)
+    def attend_queries(d, lanes=(0, 1)):
+        lane_here = (2 * group + core + d < 2 * groups) & (
+            (core == lanes[0]) | (core == lanes[-1])
+        )
+
+        @pl.when(lane_here)
         def _():
             queries = qd_buf[d + core, 0]
             grads = qd_buf[d + core, 1]
@@ -580,13 +589,13 @@
             dk_acc[...] += dot(grad_logit, queries)
             dv_acc[...] += dot(weights, grads)
 
-    def take_shared_keys(d):
-        for lane in range(2):
+    def take_shared_keys(d, lanes=(0, 1)):
+        for lane in lanes:
             m = (d + 1 - lane) // 2
             act_if(share_comes(0, m) & (core == lane), share_in(0, m), "wait_recv")
 
-    def take_shared_queries(d):
-        for lane in range(2):
+    def take_shared_queries(d, lanes=(0, 1)):
+        for lane in lanes:
             m = (d + lane) // 2
             for kind in (2, 4):
                 act_if(share_comes(kind, m) & (core == lane), share_in(kind, m), "wait_recv")
@@ -619,9 +628,13 @@
 
         @pl.when(group > 0)
         def _():
-            whole_out[:, :depth] = (joined[:, :depth] - depth_eye).astype(BF16)
-            whole_out[:, depth:] = joined[:, depth:].astype(BF16)
-            whole_copy().start()
+            whole_out[1] = joined[:, depth:].astype(BF16)
+            whole_copy(1).start()
+
+        @pl.when((group > 0) & (group < groups - 1))
+        def _():
+            whole_out[0] = (joined[:, :depth] - depth_eye).astype(BF16)
+            whole_copy(0).start()
 
     if groups > 1:
         w_in().wait_recv()
@@ -639,19 +652,20 @@
 
             @pl.when(group < groups - 1)
             def _():
-                whole_copy().wait_recv()
+                whole_copy(1).wait_recv()
 
             @pl.when(group == groups - 2)
             def _():
-                state_buf[...] = whole_in[:, depth:]
+                state_buf[...] = whole_in[1]
 
             @pl.when(group < groups - 2)
             def _():
+                whole_copy(0).wait_recv()
                 carry_copy().wait_recv()
                 carried = carry_in[...]
                 state_buf[...] = (
                     carried.astype(F32)
-                    + (dot(whole_in[:, :depth], carried) + whole_in[:, depth:].astype(F32))
+                    + (dot(whole_in[0], carried) + whole_in[1].astype(F32))
                 ).astype(BF16)
 
             state = state_buf[...]
@@ -664,9 +678,9 @@
                 carry_out[...] = start_of(0)
                 carry_copy().start()
 
-            for r in range(size - 1):
-                adj_out[r] = start_of(r + 1)
             for r in range(size):
+                if r < size - 1:
+                    adj_out[r] = start_of(r + 1)
                 act_if(rank != r, adj_copy(r), "start")
             adj_in[place] = adj_out[rank]
 
@@ -698,18 +712,21 @@
 
     pl.when(group == 0)(send_queries)
     for m in range(2, steps + 1):
+        take_shared_queries(2 * m - 1, (0,))
+        attend_queries(2 * m - 1, (0,))
+        take_shared_keys(2 * m - 1, (1,))
+        attend_keys(2 * m - 1, (1,))
         arrive((0, 2, 1, 3, 4), m, lambda kind: True)
         share_all(KEYS + QUERIES, m)
-    for d in range(3, reach + 1):
-        if d % 2:
-            take_shared_keys(d)
-        attend_keys(d)
+        attend_keys(2 * m)
+        take_shared_keys(2 * m - 1, (0,))
+        attend_keys(2 * m - 1, (0,))
 
     pl.when(group > 0)(send_queries)
-    for d in range(3, reach + 1):
-        if d % 2:
-            take_shared_queries(d)
-        attend_queries(d)
+    for m in range(2, steps + 1):
+        attend_queries(2 * m)
+        take_shared_queries(2 * m - 1, (1,))
+        attend_queries(2 * m - 1, (1,))
     grad_out[1] = blocks_of(dk_acc[...] * scaling)
     grad_out[2] = blocks_of(dv_acc[...])
     send_back(1)
@@ -808,7 +825,8 @@
         w_spread(j).wait_send()
     for h in range(heads):
         act_if(heads * core + h != rank, ab_copy(h), "wait_send")
-    act_if(composer & (group > 0), whole_copy(), "wait_send")
+    act_if(composer & (group > 0), whole_copy(1), "wait_send")
+    act_if(composer & (group > 0) & (group < groups - 1), whole_copy(0), "wait_send")
     act_if(composer & (group > 1), carry_copy(), "wait_send")
     for r in range(size):
         act_if(composer & (rank != r), adj_copy(r), "wait_send")
@@ -872,8 +890,8 @@
             pltpu.VMEM((size, depth, depth), BF16),
             pltpu.VMEM((size, depth, depth), BF16),
             pltpu.VMEM((size, depth, depth), F32),
-            pltpu.VMEM((depth, 2 * depth), BF16),
-            pltpu.VMEM((depth, 2 * depth), BF16),
+            pltpu.VMEM((2, depth, depth), BF16),
+            pltpu.VMEM((2, depth, depth), BF16),
             pltpu.VMEM((depth, depth), BF16),
             pltpu.VMEM((depth, depth), BF16),
             pltpu.VMEM((size, depth, depth), BF16),
@@ -891,7 +909,7 @@
             dma((3,)), dma((steps + 1, 3)),
             dma((max(groups - 1, 1),)), dma, dma((size - 1,)), dma,
             dma((heads,)), dma,
-            dma, dma, dma, dma,
+            dma((2,)), dma((2,)), dma, dma,
             dma((heads,)),
             dma((2,)),
             dma((others,)),

time: 27.5 us -> 27.3 us (level)
  no operation moved by 1% of the time
where the time goes in v5:
time: 27.3 us; the launch traced here: 27.2 us
  Pallas kernels  26.5 us (97%)
  between operations  0.65 us (2%)
    pallas_call x1, Pallas kernels, per_device(): pl.pallas_call(functools.partial(kernel, n, head_n), out_shape=(pltpu.VME...  25.7 us
    pallas_call x1, Pallas kernels, per_device(): pl.pallas_call(hand_over, out_shape=[jax.ShapeDtypeStruct(item.shape, ite...  0.78 us

profile of v5, /device:TPU:0, one launch (start us, length us, event | category | flops | bytes accessed | tf_op | source)
XLA Modules:
  0.0 27.2 jit_solution(5303987989470382838)
XLA Ops:
  0.6 25.7 %layer_backward.1 = (bf16[128,256]{1,0:T(8,128)(2,1)S(1)}, bf16[256,128]{1,0:T(8,128)(2,1)S(1)}, bf16[128,256]{1,0:T(8,128)(2,1)S(1)}, bf16[128,256]{1,0:T(8,128...) custom-call(bf16[128,256]{1,0:T(8,128)(2,1)} %q_hbm.1, ...), custom_call_target="tpu_custom_call" | custom-call | tf_op jit(solution)/shard_map/layer_backward/pallas_call | solution.py:869
  26.4 0.8 %hand_over.1 = (bf16[128,256]{1,0:T(8,128)(2,1)}, bf16[256,128]{1,0:T(8,128)(2,1)}, bf16[128,256]{1,0:T(8,128)(2,1)}, bf16[128,256]{1,0:T(8,128)(2,1)}, bf16[128...) custom-call(bf16[128,256]{1,0:T(8,128)(2,1)S(1)} %get-tuple-element.14.refs_0_, ...), custom_call_target="tpu_custom_call" | custom-call | tf_op jit(solution)/shard_map/hand_over/pallas_call | solution.py:923

commit v6 on v5

--- a/solution.py
+++ b/solution.py
@@ -678,9 +678,11 @@
                 carry_out[...] = start_of(0)
                 carry_copy().start()
 
-            for r in range(size):
-                if r < size - 1:
-                    adj_out[r] = start_of(r + 1)
+            adj_out[0] = start_of(1)
+            act_if(rank != 0, adj_copy(0), "start")
+            for r in range(1, size - 1):
+                adj_out[r] = start_of(r + 1)
+            for r in range(1, size):
                 act_if(rank != r, adj_copy(r), "start")
             adj_in[place] = adj_out[rank]
 

time: 27.3 us -> 27.3 us (level)
  no operation moved by 1% of the time
where the time goes in v6:
time: 27.3 us; the launch traced here: 27.2 us
  Pallas kernels  26.5 us (97%)
  between operations  0.65 us (2%)
    pallas_call x1, Pallas kernels, per_device(): pl.pallas_call(functools.partial(kernel, n, head_n), out_shape=(pltpu.VME...  25.7 us
    pallas_call x1, Pallas kernels, per_device(): pl.pallas_call(hand_over, out_shape=[jax.ShapeDtypeStruct(item.shape, ite...  0.78 us

profile of v6, /device:TPU:0, one launch (start us, length us, event | category | flops | bytes accessed | tf_op | source)
XLA Modules:
  0.0 27.2 jit_solution(14456718833814596937)
XLA Ops:
  0.6 25.7 %layer_backward.1 = (bf16[128,256]{1,0:T(8,128)(2,1)S(1)}, bf16[256,128]{1,0:T(8,128)(2,1)S(1)}, bf16[128,256]{1,0:T(8,128)(2,1)S(1)}, bf16[128,256]{1,0:T(8,128...) custom-call(bf16[128,256]{1,0:T(8,128)(2,1)} %q_hbm.1, ...), custom_call_target="tpu_custom_call" | custom-call | tf_op jit(solution)/shard_map/layer_backward/pallas_call | solution.py:871
  26.4 0.8 %hand_over.1 = (bf16[128,256]{1,0:T(8,128)(2,1)}, bf16[256,128]{1,0:T(8,128)(2,1)}, bf16[128,256]{1,0:T(8,128)(2,1)}, bf16[128,256]{1,0:T(8,128)(2,1)}, bf16[128...) custom-call(bf16[128,256]{1,0:T(8,128)(2,1)S(1)} %get-tuple-element.14.refs_0_, ...), custom_call_target="tpu_custom_call" | custom-call | tf_op jit(solution)/shard_map/hand_over/pallas_call | solution.py:925
